TPU v7x, 128 devices: a whole 4x4x4 slice. The times are simulated.
128 devices in a mesh: dp: 8 (over z, core), expert: 16 (over y, x).
Axes of the slice: x: 4, y: 4, z: 4, core: 2. Of those that a mesh axis runs over, the one named last changes fastest.
Arguments:
- tokens: bfloat16 [16384, 4096], P(('dp', 'expert')), may hold values from -6 to 6
- cotangent: bfloat16 [16384, 4096], P(('dp', 'expert')), may hold values from -0.796875 to 0.796875
- router_probs: float32 [16384, 4], P(('dp', 'expert')), may hold values from 0.1 to 1
- routing: int32 [16384, 4], P(('dp', 'expert')), may hold values from 0 to 127, all different within a row
- hot_marks: int32 [128], replicated, may hold values from 0 to 1, as said below
- cap_counts: int32 [128], replicated, may hold values from 2 to 4, as said below
- gate_up: bfloat16 [128, 2, 4096, 768], P(('dp', 'expert')), may hold values from -0.09375 to 0.09375
- adapter_in: bfloat16 [128, 32, 768], P(('dp', 'expert')), may hold values from -0.21875 to 0.21875
- adapter_out: bfloat16 [128, 32, 4096], P(('dp', 'expert')), may hold values from -0.09375 to 0.09375
Outputs:
- in_gradient: float32 [128, 32, 768], P(('dp', 'expert'))
- out_gradient: float32 [128, 32, 4096], P(('dp', 'expert'))
Inputs may be any that keep to these rules, and one draw needn't show every extreme that they name: `routing`: each token names 4 different experts. `hot_marks`: of every two experts whose numbers differ only in the bit of value 16 / 2, exactly one is marked. `cap_counts`: some expert's count equals 4.
All inputs are finite; a program needn't handle non-finite values.
Results may differ from a plain program's by a relative error of at most 0.005.
Values may be sent and summed in bfloat16 or wider, within the bound.
No kernel may reach another device: no remote copies, remote signals or barrier semaphores. Data moves between devices by JAX's collectives and lax.ppermute only.
A program may use at most 192 MiB of HBM per device.

v0:
```python
import jax
import jax.numpy as jnp
from jax import lax
from jax.sharding import PartitionSpec as P

adapter_scale_factor = 2.0


def partner(block, axis, apart):
    count = lax.axis_size(axis)
    route = []
    for low in range(count):
        high = low | 1 << apart
        if high != low and high < count:
            route += [(low, high), (high, low)]
    return lax.ppermute(block, axis, route)


def hidden_units(inputs, weights):
    gate_out = jnp.dot(inputs, weights[0], preferred_element_type=jnp.float32)
    up_out = jnp.dot(inputs, weights[1], preferred_element_type=jnp.float32)
    return (jax.nn.silu(gate_out) * up_out).astype(jnp.bfloat16)


def adapter_grads(hidden_state_rows, scaled_adapter_output, adapter_down_matrix, adapter_up_matrix):
    rank_projected_rows = (
        adapter_scale_factor
        * jnp.einsum(
            "pn,cn->pc", hidden_state_rows, adapter_down_matrix, preferred_element_type=jnp.float32
        )
    ).astype(jnp.bfloat16)
    rank_gradient_rows = (
        adapter_scale_factor
        * jnp.einsum(
            "vw,cw->vc",
            scaled_adapter_output,
            adapter_up_matrix,
            preferred_element_type=jnp.float32,
        )
    ).astype(jnp.bfloat16)
    grad_first = jnp.einsum(
        "mr,mf->rf", rank_gradient_rows, hidden_state_rows, preferred_element_type=jnp.float32
    )
    grad_second = jnp.einsum(
        "mr,md->rd", rank_projected_rows, scaled_adapter_output, preferred_element_type=jnp.float32
    )
    return (grad_first, grad_second)


def body(
    tokens,
    cotangent,
    router_probs,
    routing,
    hot_marks,
    cap_counts,
    gate_up,
    adapter_in,
    adapter_out,
):
    tok_count, model_width = tokens.shape
    top_count = routing.shape[1]
    expert_total = cap_counts.shape[0]
    capacity = tok_count * top_count // expert_total
    half_cap = capacity // 2
    pair_count = tok_count * top_count
    hidden_width = gate_up.shape[3]
    rank_width = adapter_in.shape[1]
    n_expert = lax.axis_size("expert")
    flat_route = routing.reshape(pair_count)
    expert_ids = jnp.arange(expert_total, dtype=jnp.int32)
    onehot = (flat_route[:, None] == expert_ids[None, :]).astype(jnp.int32)
    order_rank = jnp.sum((jnp.cumsum(onehot, axis=0) - onehot) * onehot, axis=1)
    own_cap = jnp.sum(onehot * cap_counts[None, :], axis=1)
    is_marked = jnp.sum(onehot * hot_marks[None, :], axis=1)
    first_block = order_rank < own_cap
    second_block = (is_marked == 1) & (order_rank >= own_cap) & (order_rank < own_cap + capacity)
    offset = order_rank - own_cap
    per_dest = capacity + half_cap
    extra_dest = jnp.where(
        offset < half_cap, flat_route, jnp.bitwise_xor(flat_route, n_expert // 2)
    )
    extra_pos = capacity + jnp.remainder(offset, half_cap)
    slot_total = expert_total * per_dest
    slot_index = jnp.where(
        first_block,
        order_rank * expert_total + flat_route,
        jnp.where(second_block, extra_pos * expert_total + extra_dest, slot_total),
    )
    pair_ids = jnp.arange(pair_count, dtype=jnp.int32)
    slot_source = (
        jnp.full((slot_total + 1,), -1, jnp.int32).at[slot_index].set(pair_ids)[:slot_total]
    )
    valid_slots = slot_source >= 0
    safe_ids = jnp.maximum(slot_source, 0)
    token_ids = safe_ids // top_count
    factor = jnp.where(valid_slots, router_probs.reshape(pair_count)[safe_ids], 0.0)
    token_rows = jnp.where(valid_slots[:, None], tokens[token_ids], jnp.zeros((), jnp.bfloat16))
    scaled_rows = (factor[:, None] * cotangent[token_ids].astype(jnp.float32)).astype(jnp.bfloat16)
    shaped_rows = token_rows.reshape(per_dest, expert_total, model_width)
    shaped_scaled = scaled_rows.reshape(per_dest, expert_total, model_width)
    arrived_rows, arrived_scaled = (
        lax.all_to_all(shaped_rows, ("dp", "expert"), split_axis=1, concat_axis=1, tiled=True),
        lax.all_to_all(shaped_scaled, ("dp", "expert"), split_axis=1, concat_axis=1, tiled=True),
    )
    first_inputs = arrived_rows[:capacity].reshape(capacity * expert_total, model_width)
    first_scaled = arrived_scaled[:capacity].reshape(capacity * expert_total, model_width)
    extra_inputs = arrived_rows[capacity:].reshape(
        (per_dest - capacity) * expert_total, model_width
    )
    extra_scaled = arrived_scaled[capacity:].reshape(
        (per_dest - capacity) * expert_total, model_width
    )
    own_weights = gate_up[0]
    own_first = adapter_in[0]
    own_second = adapter_out[0]
    own_hidden = hidden_units(first_inputs, own_weights)
    grad_first, grad_second = adapter_grads(own_hidden, first_scaled, own_first, own_second)
    swap_bit = n_expert.bit_length() - 2
    own_index = lax.axis_index("dp") * n_expert + lax.axis_index("expert")
    own_marked = lax.dynamic_index_in_dim(hot_marks, own_index, 0, keepdims=False) == 1
    packed = jnp.concatenate(
        [own_weights.reshape(-1), own_first.reshape(-1), own_second.reshape(-1)]
    )
    partner_pack = partner(packed, "expert", swap_bit)
    work_pack = jnp.where(own_marked, packed, partner_pack)
    weight_size = 2 * model_width * hidden_width
    first_size = rank_width * hidden_width
    work_weights = work_pack[:weight_size].reshape(2, model_width, hidden_width)
    work_first = work_pack[weight_size : weight_size + first_size].reshape(rank_width, hidden_width)
    work_second = work_pack[weight_size + first_size :].reshape(rank_width, model_width)
    extra_hidden = hidden_units(extra_inputs, work_weights)
    extra_first, extra_second = adapter_grads(extra_hidden, extra_scaled, work_first, work_second)
    partial_pack = jnp.concatenate([extra_first.reshape(-1), extra_second.reshape(-1)])
    kept_part = jnp.where(own_marked, partial_pack, 0.0)
    sent_part = jnp.where(own_marked, 0.0, partial_pack)
    returned = partner(sent_part, "expert", swap_bit)
    total_part = kept_part + returned
    grad_first = grad_first + total_part[:first_size].reshape(rank_width, hidden_width)
    grad_second = grad_second + total_part[first_size:].reshape(rank_width, model_width)
    return (grad_first[None], grad_second[None])


def solution(mesh):
    in_specs = (
        P(("dp", "expert"), None),
        P(("dp", "expert"), None),
        P(("dp", "expert"), None),
        P(("dp", "expert"), None),
        P(),
        P(),
        P(("dp", "expert"), None, None, None),
        P(("dp", "expert"), None, None),
        P(("dp", "expert"), None, None),
    )
    out_specs = (P(("dp", "expert"), None, None), P(("dp", "expert"), None, None))
    return jax.shard_map(body, mesh=mesh, in_specs=in_specs, out_specs=out_specs, check_vma=False)
```

profile of v0, /device:TPU:5, one launch (start us, length us, event | category | flops | bytes accessed | tf_op | source)
XLA Modules:
  0.0 616.9 jit_solution(6312010830588352964)
XLA Ops:
  4.3 2.4 scatter_custom_fusion
  6.8 5.0 gather_fusion
  11.9 5.7 gather_fusion.2
  17.6 9.9 %copy_select_fusion = bf16[6,128,4096]{2,0,1:T(8,128)(2,1)} fusion(bf16[6,128,4096]{2,1,0:T(8,128)(2,1)} %bitcast.75, pred[6,128]{0,1:T(8,128)(4,1)S(1)} %copy.34), kind=kLoop, calls=%fused_computation.7 | loop fusion | flops 3145728 | bytes 12583680 | tf_op jit(solution)/shard_map/jit(_where)/select_n | solution.py:98
  27.6 11.2 %all-to-all-start.1 = ((bf16[6,128,4096]{2,0,1:T(8,128)(2,1)}), bf16[6,128,4096]{2,0,1:T(8,128)(2,1)}, u32[]{:S(2)}, u32[]{:S(2)}) async-start(bf16[6,128,4096]{2,0,1:T(8,128)(2,1)} %copy_select_fusion), calls=%async_computation.1 | async-start | bytes 16777216 | tf_op jit(solution)/shard_map/all_to_all | solution.py:103
  39.0 22.0 %reshape_squeeze.9 = bf16[6291456]{0:T(1024)(128)(2,1)} reshape(bf16[1,2,4096,768]{3,2,1,0:T(8,128)(2,1)} %param.15) | data formatting | bytes 25165824 | tf_op jit(solution)/shard_map/reshape;squeeze | solution.py:123
  61.0 10.5 %constant_dynamic-update-slice_fusion.3 = bf16[6447104]{0:T(1024)(128)(2,1)} fusion(bf16[6291456]{0:T(1024)(128)(2,1)} %reshape_squeeze.9), kind=kLoop, calls=%fused_computation.63 | loop fusion | bytes 25165824
  72.9 2.9 collective-permute-start
  75.9 5.7 gather_fusion.1
  81.6 9.1 %convert.1 = f32[6,128,4096]{2,1,0:T(8,128)} convert(bf16[6,128,4096]{2,1,0:T(8,128)(2,1)} %bitcast.76) | non-fusion elementwise | flops 3145728 | bytes 18874368 | tf_op jit(solution)/shard_map/convert_element_type | solution.py:99
  90.8 14.9 %fusion = bf16[6,128,4096]{2,0,1:T(8,128)(2,1)} fusion(f32[6,128,4096]{2,1,0:T(8,128)} %convert.1, f32[6,128]{0,1:T(8,128)S(1)} %copy.31), kind=kLoop, calls=%fused_computation.5 | loop fusion | flops 6291456 | bytes 18877440 | tf_op jit(solution)/shard_map/convert_element_type | solution.py:99
  105.7 38.3 %all-to-all-done.1 = bf16[6,128,4096]{2,0,1:T(8,128)(2,1)} async-done(((bf16[6,128,4096]{2,0,1:T(8,128)(2,1)}), bf16[6,128,4096]{2,0,1:T(8,128)(2,1)}, u32[]{:S(2)}, u32[]{:S(2)}) %all-to-all-start.1) | async-done | bytes 6291488 | tf_op jit(solution)/shard_map/all_to_all | solution.py:103
  143.9 273.7 %all-to-all-start = ((bf16[6,128,4096]{2,0,1:T(8,128)(2,1)}), bf16[6,128,4096]{2,0,1:T(8,128)(2,1)}, u32[]{:S(2)}, u32[]{:S(2)}) async-start(bf16[6,128,4096]{2,0,1:T(8,128)(2,1)} %fusion), calls=%async_computation | async-start | bytes 16777216 | tf_op jit(solution)/shard_map/all_to_all | solution.py:104
  418.9 5.5 slice.107
  424.4 4.3 copy.40
  428.7 6.0 slice.110
  434.6 2.6 copy.42
  437.3 85.3 %all-to-all-done = bf16[6,128,4096]{2,0,1:T(8,128)(2,1)} async-done(((bf16[6,128,4096]{2,0,1:T(8,128)(2,1)}), bf16[6,128,4096]{2,0,1:T(8,128)(2,1)}, u32[]{:S(2)}, u32[]{:S(2)}) %all-to-all-start) | async-done | bytes 6291488 | tf_op jit(solution)/shard_map/all_to_all | solution.py:104
  522.5 5.5 slice.106
  528.0 4.8 copy.39
  532.8 6.1 slice.108
  540.3 6.1 fusion.3
  546.4 4.4 multiply_convert_fusion
  550.8 7.1 %broadcast_select_fusion = bf16[6447104]{0:T(1024)(128)(2,1)S(1)} fusion(bf16[6447104]{0:T(1024)(128)(2,1)} %constant_dynamic-update-slice_fusion, bf16[6447104]{0:T(1024)(128)(2,1)} %collective-permute-done, pred[]{:T(512)} %bitcast.15), kind=kLoop, calls=%fused_computation.6 | loop fusion | flops 6447104 | bytes 38682624 | tf_op jit(solution)/shard_map/jit(_where)/select_n | solution.py:126
  558.0 4.8 fusion.40
  563.4 11.6 %slice.92 = bf16[4096,768]{1,0:T(8,128)(2,1)} reshape(bf16[3145728]{0:T(1024)(128)(2,1)} %get-tuple-element.7) | data formatting | bytes 12582912 | tf_op jit(solution)/shard_map/slice | solution.py:20
  575.1 11.8 %slice.94 = bf16[4096,768]{1,0:T(8,128)(2,1)} reshape(bf16[3145728]{0:T(1024)(128)(2,1)} %get-tuple-element.8) | data formatting | bytes 12582912 | tf_op jit(solution)/shard_map/slice | solution.py:21
  586.9 5.3 fusion.41
  592.7 1.9 multiply_convert_fusion.1
  598.3 3.6 fusion.12
  602.0 3.8 fusion.11
  605.7 8.1 %collective-permute-done.1 = f32[155648]{0:T(1024)} collective-permute-done((f32[155648]{0:T(1024)}, f32[155648]{0:T(1024)}, u32[]{:S(2)}, u32[]{:S(2)}) %collective-permute-start.1) | collective-permute-done | bytes 622624 | tf_op jit(solution)/shard_map/ppermute | solution.py:16
  (76 shorter events, 15.0 us)
Async XLA Ops:
  0.6 11.3 %copy-start = (bf16[128,4096]{1,0:T(8,128)(2,1)S(1)}, bf16[128,4096]{1,0:T(8,128)(2,1)}, u32[]{:S(2)}) copy-start(bf16[128,4096]{1,0:T(8,128)(2,1)} %param.9) | copy-start | bytes 3145732
  27.6 11.3 %copy-start.8 = (bf16[1,32,768]{2,1,0:T(8,128)(2,1)S(1)}, bf16[1,32,768]{2,1,0:T(8,128)(2,1)}, u32[]{:S(2)}) copy-start(bf16[1,32,768]{2,1,0:T(8,128)(2,1)} %param.16) | copy-start | bytes 147460
  27.6 11.3 %copy-start.7 = (bf16[1,32,4096]{2,1,0:T(8,128)(2,1)S(1)}, bf16[1,32,4096]{2,1,0:T(8,128)(2,1)}, u32[]{:S(2)}) copy-start(bf16[1,32,4096]{2,1,0:T(8,128)(2,1)} %param.17) | copy-start | bytes 786436
  27.6 116.3 %all-to-all-start.1 = ((bf16[6,128,4096]{2,0,1:T(8,128)(2,1)}), bf16[6,128,4096]{2,0,1:T(8,128)(2,1)}, u32[]{:S(2)}, u32[]{:S(2)}) async-start(bf16[6,128,4096]{2,0,1:T(8,128)(2,1)} %copy_select_fusion), calls=%async_computation.1 | async-start | bytes 16777216 | tf_op jit(solution)/shard_map/all_to_all | solution.py:103
  61.0 14.9 %copy-start.2 = (bf16[128,4096]{1,0:T(8,128)(2,1)S(1)}, bf16[128,4096]{1,0:T(8,128)(2,1)}, u32[]{:S(2)}) copy-start(bf16[128,4096]{1,0:T(8,128)(2,1)} %param.10) | copy-start | bytes 3145732
  72.9 477.9 %collective-permute-start = (bf16[6447104]{0:T(1024)(128)(2,1)}, bf16[6447104]{0:T(1024)(128)(2,1)}, u32[]{:S(2)}, u32[]{:S(2)}) collective-permute-start(bf16[6447104]{0:T(1024)(128)(2,1)} %constant_dynamic-update-slice_fusion), channel_id=1, source_target_pairs={{0,8},{8,0},{1,9},{9,1},{2,10},{10,2},{3,11},{11,3},{4,12},{12,4},... | collective-permute-start | bytes 38682632 | tf_op jit(solution)/shard_map/ppermute | solution.py:16
  105.7 312.0 %copy-start.9 = (s32[128]{0:T(128)S(1)}, s32[128]{0:T(128)}, u32[]{:S(2)}) copy-start(s32[128]{0:T(128)} %param.13) | copy-start | bytes 1540
  143.9 378.6 %all-to-all-start = ((bf16[6,128,4096]{2,0,1:T(8,128)(2,1)}), bf16[6,128,4096]{2,0,1:T(8,128)(2,1)}, u32[]{:S(2)}, u32[]{:S(2)}) async-start(bf16[6,128,4096]{2,0,1:T(8,128)(2,1)} %fusion), calls=%async_computation | async-start | bytes 16777216 | tf_op jit(solution)/shard_map/all_to_all | solution.py:104
  532.8 7.5 %copy-start.4 = (bf16[4,128,4096]{2,1,0:T(8,128)(2,1)S(1)}, bf16[4,128,4096]{2,1,0:T(8,128)(2,1)}, u32[]{:S(2)}) copy-start(bf16[4,128,4096]{2,1,0:T(8,128)(2,1)} %copy.40) | copy-start | bytes 12582916
  538.9 7.5 %slice-start = ((s8[12582912]{0:T(1024)(128)(4,1)}), s8[4194304]{0:T(1024)(128)(4,1)S(1)}, s32[]{:S(2)}) async-start(s8[12582912]{0:T(1024)(128)(4,1)} %bitcast.79), calls=%async_computation.2 | async-start | bytes 8388608
  540.2 6.1 slice-start.1
  540.3 6.1 slice-start.2
  586.9 5.4 copy-start.3
  586.9 5.8 copy-start.6
  597.2 4.7 copy-start.5
  598.3 15.5 %collective-permute-start.1 = (f32[155648]{0:T(1024)}, f32[155648]{0:T(1024)}, u32[]{:S(2)}, u32[]{:S(2)}) collective-permute-start(f32[155648]{0:T(1024)} %broadcast_select_fusion.1), channel_id=1, source_target_pairs={{0,8},{8,0},{1,9},{9,1},{2,10},{10,2},{3,11},{11,3},{4,12},{12,4},... | collective-permute-start | bytes 1867784 | tf_op jit(solution)/shard_map/ppermute | solution.py:16
  598.3 18.4 %copy-start.1 = (bf16[128,4096]{1,0:T(8,128)(2,1)S(1)}, bf16[128,4096]{1,0:T(8,128)(2,1)}, u32[]{:S(2)}) copy-start(bf16[128,4096]{1,0:T(8,128)(2,1)} %param.9) | copy-start | bytes 3145732
where the time goes:
time: 626 us; the launch traced here: 617 us
  starting transfers between devices  288 us (46%)
  waiting for transfers between devices  132 us (21%)
  local copies, waits for them, and re-layouts  122 us (19%)
  other arithmetic  46 us (7%)
  matrix products  27.7 us (4%)
    all_to_all x1, starting transfers between devices, body(): lax.all_to_all(shaped_scaled, ('dp', 'expert'), split_axis=1, concat_axis...  274 us
    all_to_all x1, waiting for transfers between devices, body(): lax.all_to_all(shaped_scaled, ('dp', 'expert'), split_axis=1, concat_axis...  85.3 us
    all_to_all x1, waiting for transfers between devices, body(): lax.all_to_all(shaped_rows, ('dp', 'expert'), split_axis=1, concat_axis=1...  38.3 us
    unnamed x38, local copies, waits for them, and re-layouts  26.5 us
    another operation x1, local copies, waits for them, and re-layouts, body(): own_weights.reshape(-1)  22 us
    slice x2, local copies, waits for them, and re-layouts, hidden_units(): gate_out = jnp.dot(inputs, weights[0], preferred_element_type=jnp.float32)  16.4 us
    convert_element_type x1, other arithmetic, body(): (factor[:, None] * cotangent[token_ids].astype(jnp.float32)).astype(jnp.b...  14.9 us
  transfers between devices with their start and end apart: 4, of which 3 were waited for; matrix products, arithmetic and copies ran while one was open for 19% of the time, Pallas kernels for 0%

commit v1 on v0

v1 whole, which is shorter than its diff:
```python
import jax
import jax.numpy as jnp
from jax import lax
from jax.sharding import PartitionSpec as P

SCALE = 2.0
SLOTS = 8
AXES = ("dp", "expert")


def slot_masks(routing, router_probs, hot_marks, cap_counts):
    tok_count, top_count = routing.shape
    experts = cap_counts.shape[0]
    expert_ids = jnp.arange(experts, dtype=jnp.int32)
    limit = cap_counts + (tok_count * top_count // experts) * hot_marks
    hit = routing.T[:, None, :] == expert_ids[None, :, None]
    member = jnp.any(hit, axis=0)
    weight = jnp.sum(jnp.where(hit, router_probs.T[:, None, :], 0.0), axis=0)
    before = lax.broadcasted_iota(jnp.int32, (tok_count, tok_count), 0) < lax.broadcasted_iota(
        jnp.int32, (tok_count, tok_count), 1
    )
    rank = jnp.dot(
        member.astype(jnp.bfloat16), before.astype(jnp.bfloat16), preferred_element_type=jnp.float32
    ).astype(jnp.int32)
    rank = jnp.where(member & (rank < limit[:, None]), rank, -1)
    slots = lax.broadcasted_iota(jnp.int32, (experts, SLOTS, tok_count), 1)
    sel = rank[:, None, :] == slots
    factor = jnp.sum(jnp.where(sel, weight[:, None, :], 0.0), axis=2)
    return sel, factor


def body(
    tokens, cotangent, router_probs, routing, hot_marks, cap_counts, gate_up, adapter_in, adapter_out
):
    tok_count, model_width = tokens.shape
    experts = cap_counts.shape[0]
    rows = experts * SLOTS
    sel, factor = slot_masks(routing, router_probs, hot_marks, cap_counts)
    pick = sel.reshape(rows, tok_count).astype(jnp.bfloat16)
    sent_tokens = jnp.dot(pick, tokens, preferred_element_type=jnp.float32).astype(jnp.bfloat16)
    inputs = lax.all_to_all(
        sent_tokens.reshape(experts, SLOTS, model_width), AXES, split_axis=0, concat_axis=0, tiled=True
    ).reshape(rows, model_width)
    picked = jnp.dot(pick, cotangent, preferred_element_type=jnp.float32)
    sent_scaled = (factor.reshape(rows, 1) * picked).astype(jnp.bfloat16)
    scaled = lax.all_to_all(
        sent_scaled.reshape(experts, SLOTS, model_width), AXES, split_axis=0, concat_axis=0, tiled=True
    ).reshape(rows, model_width)
    gate_out = jnp.dot(inputs, gate_up[0, 0], preferred_element_type=jnp.float32)
    up_out = jnp.dot(inputs, gate_up[0, 1], preferred_element_type=jnp.float32)
    hidden = (jax.nn.silu(gate_out) * up_out).astype(jnp.bfloat16)
    low = (
        SCALE * jnp.einsum("nf,rf->nr", hidden, adapter_in[0], preferred_element_type=jnp.float32)
    ).astype(jnp.bfloat16)
    back = (
        SCALE * jnp.einsum("nd,rd->nr", scaled, adapter_out[0], preferred_element_type=jnp.float32)
    ).astype(jnp.bfloat16)
    in_grad = jnp.einsum("nr,nf->rf", back, hidden, preferred_element_type=jnp.float32)
    out_grad = jnp.einsum("nr,nd->rd", low, scaled, preferred_element_type=jnp.float32)
    return in_grad[None], out_grad[None]


def solution(mesh):
    in_specs = (
        P(AXES, None),
        P(AXES, None),
        P(AXES, None),
        P(AXES, None),
        P(),
        P(),
        P(AXES, None, None, None),
        P(AXES, None, None),
        P(AXES, None, None),
    )
    out_specs = (P(AXES, None, None), P(AXES, None, None))
    return jax.shard_map(body, mesh=mesh, in_specs=in_specs, out_specs=out_specs, check_vma=False)
```

time: 626 us -> 249 us (0.40); the launches traced: 617 us -> 249 us
  starting transfers between devices: 288 us -> 17.4 us
  local copies, waits for them, and re-layouts: 122 us -> 0.22 us
  waiting for transfers between devices: 132 us -> 183 us
  other arithmetic: 46 us -> 1.73 us
  matrix products: 27.7 us -> 46 us
    all_to_all x2, starting transfers between devices: 285 us -> 17.4 us  [the longest x1 11.2 us: body(): lax.all_to_all(sent_tokens.reshape(experts, SLOTS, model_width), AXES, sp...]
    all_to_all x2, waiting for transfers between devices: 124 us -> 183 us  [the longest x1 99.7 us: body(): lax.all_to_all(sent_tokens.reshape(experts, SLOTS, model_width), AXES, sp...]
    slice x13 -> x0, local copies, waits for them, and re-layouts: 51.4 us -> none  [the longest x2 16.4 us: hidden_units(): gate_out = jnp.dot(inputs, weights[0], preferred_element_type=jnp.float32)]
    unnamed x38 -> x12, local copies, waits for them, and re-layouts: 26.5 us -> 0.03 us
    convert_element_type x2 -> x0, other arithmetic: 24 us -> none  [the longest x1 14.9 us: body(): (factor[:, None] * cotangent[token_ids].astype(jnp.float32)).astype(jnp.b...]
    another operation x5 -> x0, local copies, waits for them, and re-layouts: 22.1 us -> none  [the longest x1 22 us: body(): own_weights.reshape(-1)]
    dot_general x8 -> x7, matrix products: 27.7 us -> 46 us  [the longest x1 11.3 us: body(): jnp.dot(inputs, gate_up[0, 0], preferred_element_type=jnp.float32)]
    select_n x5 -> x0, other arithmetic: 18 us -> none  [the longest x1 9.94 us: body(): jnp.where(valid_slots[:, None], tokens[token_ids], jnp.zeros((), jnp.bflo...]
  transfers between devices with their start and end apart: 4 -> 2, of which waited for: 3 -> 2; matrix products, arithmetic and copies ran while one was open for 19% -> 11% of each run, Pallas kernels for 0% -> 0%
where the time goes in v1:
time: 249 us
  waiting for transfers between devices  183 us (73%)
  matrix products  46 us (18%)
  starting transfers between devices  17.4 us (7%)
    all_to_all x1, waiting for transfers between devices, body(): lax.all_to_all(sent_tokens.reshape(experts, SLOTS, model_width), AXES, sp...  99.7 us
    all_to_all x1, waiting for transfers between devices, body(): lax.all_to_all(sent_scaled.reshape(experts, SLOTS, model_width), AXES, sp...  82.9 us
    dot_general x1, matrix products, body(): jnp.dot(inputs, gate_up[0, 0], preferred_element_type=jnp.float32)  11.3 us
    all_to_all x1, starting transfers between devices, body(): lax.all_to_all(sent_tokens.reshape(experts, SLOTS, model_width), AXES, sp...  11.2 us
    dot_general x1, matrix products, body(): up_out = jnp.dot(inputs, gate_up[0, 1], preferred_element_type=jnp.float32)  10.9 us
    dot_general x1, matrix products, body(): jnp.einsum('nr,nf->rf', back, hidden, preferred_element_type=jnp.float32)  6.91 us
    dot_general x1, matrix products, body(): jnp.einsum('nr,nd->rd', low, scaled, preferred_element_type=jnp.float32)  6.2 us
    all_to_all x1, starting transfers between devices, body(): lax.all_to_all(sent_scaled.reshape(experts, SLOTS, model_width), AXES, sp...  6.13 us
  transfers between devices with their start and end apart: 2, of which 2 were waited for; matrix products, arithmetic and copies ran while one was open for 11% of the time, Pallas kernels for 0%

profile of v1, /device:TPU:5, one launch (start us, length us, event | category | flops | bytes accessed | tf_op | source)
XLA Modules:
  0.0 248.7 jit_solution(6195834785091898382)
XLA Ops:
  0.6 0.0 copy-start
  0.6 0.8 fusion.35
  1.5 0.1 iota.31
  1.6 0.7 multiply_add_fusion
  2.2 0.2 and_select_fusion
  2.4 0.0 copy-done
  2.4 5.6 %convert_bitcast_fusion = bf16[128,8,4096]{2,1,0:T(8,128)(2,1)} fusion(bf16[128,4096]{1,0:T(8,128)(2,1)S(1)} %copy-done, s32[1024]{0:T(1024)S(1)} %iota.31, s32[128,128]{1,0:T(8,128)S(1)} %and_select_fusion), kind=kOutput, calls=%fused_computation.9 | convolution fusion | flops 1078067200 | bytes 9506816 | tf_op jit(solution)/shard_map/dot_general | solution.py:40
  8.0 0.0 copy-start.4
  8.0 0.0 copy-start.5
  8.0 0.0 copy-start.1
  8.0 11.2 %all-to-all-start.1 = ((bf16[128,8,4096]{2,1,0:T(8,128)(2,1)}), bf16[128,8,4096]{2,1,0:T(8,128)(2,1)}, u32[]{:S(2)}, u32[]{:S(2)}) async-start(bf16[128,8,4096]{2,1,0:T(8,128)(2,1)} %convert_bitcast_fusion), calls=%async_computation.1 | async-start | bytes 16777216 | tf_op jit(solution)/shard_map/all_to_all | solution.py:41
  19.3 0.0 copy-done.4
  19.3 0.0 copy-done.5
  19.3 0.2 select_reduce_fusion
  19.5 0.1 mul.31
  19.6 0.0 copy-done.1
  19.6 5.0 %fusion.8 = bf16[128,8,4096]{2,1,0:T(8,128)(2,1)} fusion(bf16[128,4096]{1,0:T(8,128)(2,1)S(1)} %copy-done.1, f32[1024]{0:T(1024)S(1)} %mul.31, s32[1024]{0:T(1024)S(1)} %iota.31, s32[128,128]{1,0:T(8,128)S(1)} %and_select_fusion), kind=kOutput, calls=%fused_computation.10 | convolution fusion | flops 1082261504 | bytes 9510912 | tf_op jit(solution)/shard_map/dot_general | solution.py:44
  24.6 99.7 %all-to-all-done.1 = bf16[128,8,4096]{2,1,0:T(8,128)(2,1)} async-done(((bf16[128,8,4096]{2,1,0:T(8,128)(2,1)}), bf16[128,8,4096]{2,1,0:T(8,128)(2,1)}, u32[]{:S(2)}, u32[]{:S(2)}) %all-to-all-start.1) | async-done | bytes 8388640 | tf_op jit(solution)/shard_map/all_to_all | solution.py:41
  124.3 6.1 %all-to-all-start = ((bf16[128,8,4096]{2,1,0:T(8,128)(2,1)}), bf16[128,8,4096]{2,1,0:T(8,128)(2,1)}, u32[]{:S(2)}, u32[]{:S(2)}) async-start(bf16[128,8,4096]{2,1,0:T(8,128)(2,1)} %fusion.8), calls=%async_computation | async-start | bytes 16777216 | tf_op jit(solution)/shard_map/all_to_all | solution.py:46
  130.5 10.9 %fusion = f32[1024,768]{1,0:T(8,128)S(1)} fusion(bf16[128,8,4096]{2,1,0:T(8,128)(2,1)} %all-to-all-done.1, bf16[1,2,4096,768]{3,2,1,0:T(8,128)(2,1)} %param.15), kind=kOutput, calls=%fused_computation.1 | convolution fusion | flops 6442450944 | bytes 17825792 | tf_op jit(solution)/shard_map/dot_general | solution.py:50
  141.4 0.0 copy-start.3
  141.4 11.3 %multiply_convert_fusion.1 = bf16[1024,768]{1,0:T(8,128)(2,1)S(1)} fusion(f32[1024,768]{1,0:T(8,128)S(1)} %fusion, bf16[1,2,4096,768]{3,2,1,0:T(8,128)(2,1)} %param.15, bf16[128,8,4096]{2,1,0:T(8,128)(2,1)} %all-to-all-done.1), kind=kOutput, calls=%fused_computation.16 | convolution fusion | flops 6447169536 | bytes 19398656 | tf_op jit(solution)/shard_map/dot_general | solution.py:49
  152.7 0.0 copy-start.2
  152.7 82.9 %all-to-all-done = bf16[128,8,4096]{2,1,0:T(8,128)(2,1)} async-done(((bf16[128,8,4096]{2,1,0:T(8,128)(2,1)}), bf16[128,8,4096]{2,1,0:T(8,128)(2,1)}, u32[]{:S(2)}, u32[]{:S(2)}) %all-to-all-start) | async-done | bytes 8388640 | tf_op jit(solution)/shard_map/all_to_all | solution.py:46
  235.6 0.0 copy-done.3
  235.6 6.2 %fusion.13 = f32[1,32,4096]{2,1,0:T(8,128)} fusion(bf16[128,8,4096]{2,1,0:T(8,128)(2,1)} %all-to-all-done, bf16[1024,768]{1,0:T(8,128)(2,1)S(1)} %multiply_convert_fusion.1, bf16[1,32,768]{2,1,0:T(8,128)(2,1)S(1)} %copy-done.3), kind=kOutput, calls=%fused_computation.15 | convolution fusion | flops 318832640 | bytes 10534912 | tf_op jit(solution)/shard_map/nr,nd->rd/dot_general | solution.py:59
  241.8 0.0 copy-done.2
  241.8 6.9 %convolution_bitcast_fusion = f32[1,32,768]{2,1,0:T(8,128)} fusion(bf16[1024,768]{1,0:T(8,128)(2,1)S(1)} %multiply_convert_fusion.1, bf16[128,8,4096]{2,1,0:T(8,128)(2,1)} %all-to-all-done, bf16[1,32,4096]{2,1,0:T(8,128)(2,1)S(1)} %copy-done.2), kind=kOutput, calls=%fused_computation.19 | convolution fusion | flops 318832640 | bytes 10321920 | tf_op jit(solution)/shard_map/nr,nf->rf/dot_general | solution.py:58
  (2 shorter events, 0.0 us)
Async XLA Ops:
  0.6 1.8 copy-start
  8.0 11.3 %copy-start.4 = (s32[128,4]{0,1:T(4,128)S(1)}, s32[128,4]{0,1:T(4,128)}, u32[]{:S(2)}) copy-start(s32[128,4]{0,1:T(4,128)} %param.12) | copy-start | bytes 6148
  8.0 11.3 %copy-start.5 = (f32[128,4]{0,1:T(4,128)S(1)}, f32[128,4]{0,1:T(4,128)}, u32[]{:S(2)}) copy-start(f32[128,4]{0,1:T(4,128)} %param.11) | copy-start | bytes 6148
  8.0 11.6 %copy-start.1 = (bf16[128,4096]{1,0:T(8,128)(2,1)S(1)}, bf16[128,4096]{1,0:T(8,128)(2,1)}, u32[]{:S(2)}) copy-start(bf16[128,4096]{1,0:T(8,128)(2,1)} %param.10) | copy-start | bytes 3145732
  8.0 116.3 %all-to-all-start.1 = ((bf16[128,8,4096]{2,1,0:T(8,128)(2,1)}), bf16[128,8,4096]{2,1,0:T(8,128)(2,1)}, u32[]{:S(2)}, u32[]{:S(2)}) async-start(bf16[128,8,4096]{2,1,0:T(8,128)(2,1)} %convert_bitcast_fusion), calls=%async_computation.1 | async-start | bytes 16777216 | tf_op jit(solution)/shard_map/all_to_all | solution.py:41
  124.3 111.2 %all-to-all-start = ((bf16[128,8,4096]{2,1,0:T(8,128)(2,1)}), bf16[128,8,4096]{2,1,0:T(8,128)(2,1)}, u32[]{:S(2)}, u32[]{:S(2)}) async-start(bf16[128,8,4096]{2,1,0:T(8,128)(2,1)} %fusion.8), calls=%async_computation | async-start | bytes 16777216 | tf_op jit(solution)/shard_map/all_to_all | solution.py:46
  141.4 94.2 %copy-start.3 = (bf16[1,32,768]{2,1,0:T(8,128)(2,1)S(1)}, bf16[1,32,768]{2,1,0:T(8,128)(2,1)}, u32[]{:S(2)}) copy-start(bf16[1,32,768]{2,1,0:T(8,128)(2,1)} %param.16) | copy-start | bytes 147460
  152.7 89.1 %copy-start.2 = (bf16[1,32,4096]{2,1,0:T(8,128)(2,1)S(1)}, bf16[1,32,4096]{2,1,0:T(8,128)(2,1)}, u32[]{:S(2)}) copy-start(bf16[1,32,4096]{2,1,0:T(8,128)(2,1)} %param.17) | copy-start | bytes 786436

commit v2 on v1

v2 whole, which is shorter than its diff:
```python
import functools

import jax
import jax.numpy as jnp
from jax import lax
from jax.experimental import pallas as pl
from jax.experimental.pallas import tpu as pltpu
from jax.sharding import PartitionSpec as P


SCALE = 2.0
SLOTS = 8
BASE = 4
EXTRA = 2
GROUP = 16
AXES = ("dp", "expert")


def slot_table(experts, routing, probs, limit):
    tok_count = routing.shape[1]
    hit = [routing[k : k + 1, :] == experts for k in range(routing.shape[0])]
    member = sum(jnp.where(h, 1.0, 0.0) for h in hit)
    weight = sum(jnp.where(h, probs[k : k + 1, :], 0.0) for k, h in enumerate(hit))
    before = lax.broadcasted_iota(jnp.int32, (tok_count, tok_count), 0) < lax.broadcasted_iota(
        jnp.int32, (tok_count, tok_count), 1
    )
    rank = jnp.dot(
        member.astype(jnp.bfloat16),
        jnp.where(before, 1.0, 0.0).astype(jnp.bfloat16),
        preferred_element_type=jnp.float32,
    ).astype(jnp.int32)
    return jnp.where((member > 0.0) & (rank < limit), rank, -1), weight


def look_up(table, experts):
    lanes = lax.broadcasted_iota(jnp.int32, (experts.shape[0], table.shape[1]), 1)
    return jnp.sum(jnp.where(lanes == experts, table, 0), axis=1, keepdims=True)


def block_experts():
    first = pl.program_id(0) * GROUP
    return first + lax.broadcasted_iota(jnp.int32, (GROUP, 1), 0)


def spread(rank, weight, rows, parts):
    group, tok_count = rank.shape
    sublane = lax.broadcasted_iota(jnp.int32, (group, SLOTS, tok_count), 1)
    match = rank[:, None, :] == sublane // parts
    factor = jnp.sum(jnp.where(match, weight[:, None, :], 0.0), axis=2, keepdims=True)
    width = rows.shape[1] // parts
    total = jnp.zeros((group * SLOTS, width), jnp.float32)
    for part in range(parts):
        pick = jnp.where(match & (sublane % parts == part), 1.0, 0.0).astype(jnp.bfloat16)
        total += jnp.dot(
            pick.reshape(group * SLOTS, tok_count),
            rows[:, part * width : (part + 1) * width],
            preferred_element_type=jnp.float32,
        )
    return (total.reshape(group, SLOTS, width) * factor).astype(jnp.bfloat16)


def pack_first_kernel(half, room, routing, probs, marks, caps, tokens, cotangent, out):
    tok_count, width = tokens.shape
    experts = block_experts()
    marked = look_up(marks[...], experts)
    limit = look_up(caps[...], experts) + room * marked
    rank, _ = slot_table(experts, routing[...], probs[...], limit)
    sublane = lax.broadcasted_iota(jnp.int32, (GROUP, SLOTS, tok_count), 1)
    pick = jnp.where(rank[:, None, :] == sublane, 1.0, 0.0).astype(jnp.bfloat16)
    rows = jnp.dot(
        pick.reshape(GROUP * SLOTS, tok_count), tokens[...], preferred_element_type=jnp.float32
    )
    out[:, :, :width] = rows.astype(jnp.bfloat16).reshape(GROUP, SLOTS, width)
    hot = jnp.where(marked == 1, experts, experts ^ half)
    hot_rank, hot_weight = slot_table(
        hot, routing[...], probs[...], look_up(caps[...], hot) + room
    )
    hot_rank = hot_rank - jnp.where(marked == 1, BASE, BASE + EXTRA)
    out[:, :, width:] = spread(hot_rank, hot_weight, cotangent, SLOTS // EXTRA)


def pack_second_kernel(room, routing, probs, marks, caps, cotangent, out):
    experts = block_experts()
    limit = look_up(caps[...], experts) + room * look_up(marks[...], experts)
    rank, weight = slot_table(experts, routing[...], probs[...], limit)
    out[...] = spread(rank, weight, cotangent, SLOTS // BASE)


def pack(kernel, tables, arrays, width):
    experts = tables[-1].shape[1]
    operands = tables + arrays
    return pl.pallas_call(
        kernel,
        grid=(experts // GROUP,),
        in_specs=[pl.BlockSpec(x.shape, lambda i: (0, 0)) for x in operands],
        out_specs=pl.BlockSpec((GROUP, SLOTS, width), lambda i: (i, 0, 0)),
        out_shape=jax.ShapeDtypeStruct((experts, SLOTS, width), jnp.bfloat16),
    )(*operands)


def finish_kernel(base, low, hidden, own_out, grad, in_grad):
    step = pl.program_id(0)
    block, width = base.shape
    parts = SLOTS // BASE
    row = lax.broadcasted_iota(jnp.int32, (block, block), 0)
    column = lax.broadcasted_iota(jnp.int32, (block, block), 1)
    same = row // SLOTS == column // SLOTS
    widen = jnp.where(same & (row % SLOTS // parts == column % SLOTS), 1.0, 0.0).astype(low.dtype)
    narrow = jnp.where(same & (row % SLOTS * parts == column % SLOTS), 1.0, 0.0).astype(low.dtype)
    rows_low = jnp.dot(widen, low[...], preferred_element_type=jnp.float32).astype(low.dtype)
    part = lax.broadcasted_iota(jnp.int32, rows_low.shape, 0) % parts
    back = None
    for at in range(parts):
        columns = slice(at * width, (at + 1) * width)
        part_low = jnp.where(part == at, rows_low, jnp.zeros((), low.dtype))
        new = lax.dot_general(
            part_low, base[...], (((0,), (0,)), ((), ())), preferred_element_type=jnp.float32
        )
        grad[:, columns] = jnp.where(step == 0, 0.0, grad[:, columns]) + new
        half_back = lax.dot_general(
            base[...], own_out[:, columns], (((1,), (1,)), ((), ())), preferred_element_type=jnp.float32
        )
        back = half_back if back is None else back + pltpu.roll(half_back, block - at, 0)
    back = (SCALE * back).astype(jnp.bfloat16)
    back = jnp.dot(narrow, back, preferred_element_type=jnp.float32).astype(jnp.bfloat16)
    new_in = lax.dot_general(
        back, hidden[...], (((0,), (0,)), ((), ())), preferred_element_type=jnp.float32
    )
    in_grad[...] = jnp.where(step == 0, 0.0, in_grad[...]) + new_in


def finish(base, low, hidden, own_out):
    rows, width = base.shape
    rank_width, hidden_width = low.shape[1], hidden.shape[1]
    block = rows // 4
    row_block = lambda columns: pl.BlockSpec((block, columns), lambda i: (i, 0))
    kept = lambda shape: pl.BlockSpec(shape, lambda i: (0, 0))
    return pl.pallas_call(
        finish_kernel,
        grid=(rows // block,),
        in_specs=[row_block(width), row_block(rank_width), row_block(hidden_width), kept(own_out.shape)],
        out_specs=[kept(own_out.shape), kept((rank_width, hidden_width))],
        out_shape=[
            jax.ShapeDtypeStruct(own_out.shape, jnp.float32),
            jax.ShapeDtypeStruct((rank_width, hidden_width), jnp.float32),
        ],
    )(base, low, hidden, own_out)


def exchange(block):
    return lax.all_to_all(block, AXES, split_axis=0, concat_axis=0, tiled=True)


def layer(
    tokens, cotangent, router_probs, routing, hot_marks, cap_counts, gate_up, adapter_in, adapter_out
):
    model_width = tokens.shape[1]
    experts = cap_counts.shape[0]
    n_expert = lax.axis_size("expert")
    half = n_expert // 2
    pairs = [(i, i ^ half) for i in range(n_expert)]
    own_index = lax.axis_index("dp") * n_expert + lax.axis_index("expert")
    own_marked = lax.dynamic_index_in_dim(hot_marks, own_index, 0, keepdims=False) == 1
    own_in, own_out = adapter_in[0], adapter_out[0]

    partner_out = lax.ppermute(own_out, "expert", pairs)
    room = tokens.shape[0] * routing.shape[1] // experts
    tables = (routing.T, router_probs.T, hot_marks[None, :], cap_counts[None, :])
    first = pack(
        functools.partial(pack_first_kernel, half, room),
        tables,
        (tokens, cotangent),
        model_width + EXTRA * model_width // SLOTS,
    )
    first = exchange(first)
    second = pack(
        functools.partial(pack_second_kernel, room), tables, (cotangent,), BASE * model_width // SLOTS
    )
    second = exchange(second)

    inputs = first[:, :, :model_width].reshape(experts * SLOTS, model_width)
    gate_out = jnp.dot(inputs, gate_up[0, 0], preferred_element_type=jnp.float32)
    up_out = jnp.dot(inputs, gate_up[0, 1], preferred_element_type=jnp.float32)
    hidden = (jax.nn.silu(gate_out) * up_out).astype(jnp.bfloat16)
    low = (
        SCALE * jnp.einsum("nf,rf->nr", hidden, own_in, preferred_element_type=jnp.float32)
    ).astype(jnp.bfloat16)
    rank_width, hidden_width = own_in.shape
    hidden = hidden.reshape(experts, SLOTS, hidden_width)
    low = low.reshape(experts, SLOTS, rank_width)

    parts = SLOTS // EXTRA
    extra = first[:, :, model_width:].reshape(experts, EXTRA, parts, model_width // parts)
    extra = extra.reshape(experts * EXTRA, model_width)
    work_out = jnp.where(own_marked, own_out, partner_out)
    extra_back = (
        SCALE * jnp.einsum("nd,rd->nr", extra, work_out, preferred_element_type=jnp.float32)
    ).astype(jnp.bfloat16)
    extra_back = extra_back.reshape(experts, EXTRA, rank_width)
    swapped = lax.ppermute(
        jnp.where(own_marked, low[:, BASE + EXTRA :], extra_back), "expert", pairs
    )
    extra_low = jnp.where(own_marked, low[:, BASE : BASE + EXTRA], swapped)
    extra_grad = jnp.einsum(
        "nr,nd->rd",
        extra_low.reshape(experts * EXTRA, rank_width),
        extra,
        preferred_element_type=jnp.float32,
    )
    returned = lax.ppermute(extra_grad, "expert", pairs)
    hot_back = jnp.concatenate([extra_back, swapped], axis=1)
    hot_back = jnp.where(own_marked, hot_back, jnp.zeros((), jnp.bfloat16))
    in_grad = jnp.einsum(
        "sjr,sjf->rf", hot_back, hidden[:, BASE:], preferred_element_type=jnp.float32
    )

    base_grad, base_in = finish(
        second.reshape(experts * SLOTS, BASE * model_width // SLOTS),
        low.reshape(experts * SLOTS, rank_width),
        hidden.reshape(experts * SLOTS, hidden_width),
        own_out,
    )
    in_grad = base_in + in_grad
    out_grad = base_grad + jnp.where(own_marked, extra_grad + returned, 0.0)
    return in_grad[None], out_grad[None]


def solution(mesh):
    in_specs = (
        P(AXES, None),
        P(AXES, None),
        P(AXES, None),
        P(AXES, None),
        P(),
        P(),
        P(AXES, None, None, None),
        P(AXES, None, None),
        P(AXES, None, None),
    )
    out_specs = (P(AXES, None, None), P(AXES, None, None))
    return jax.shard_map(layer, mesh=mesh, in_specs=in_specs, out_specs=out_specs, check_vma=False)
```

time: 249 us -> 237 us (0.952)
  waiting for transfers between devices: 183 us -> 143 us
  Pallas kernels: 0 us -> 27 us
  matrix products: 46 us -> 27.1 us
  local copies, waits for them, and re-layouts: 0.22 us -> 8.96 us
  starting transfers between devices: 17.4 us -> 25.7 us
    all_to_all x2, waiting for transfers between devices: 183 us -> 137 us  [exchange(): return lax.all_to_all(block, AXES, split_axis=0, concat_axis=0, tiled=True)]
    pallas_call x0 -> x3, Pallas kernels: none -> 27 us  [the longest x2 18.2 us: pack(): pl.pallas_call(kernel, grid=(experts // GROUP,), in_specs=[pl.BlockSpec(x...]
    dot_general x7 -> x6, matrix products: 46 us -> 27.1 us  [the longest x1 12 us: layer(): jnp.dot(inputs, gate_up[0, 0], preferred_element_type=jnp.float32)]
    ppermute x0 -> x3, waiting for transfers between devices: none -> 6.23 us  [the longest x1 6.22 us: layer(): lax.ppermute(jnp.where(own_marked, low[:, BASE + EXTRA:], extra_back), 'e...]
    ppermute x0 -> x3, starting transfers between devices: none -> 6.06 us  [the longest x1 2.79 us: layer(): partner_out = lax.ppermute(own_out, 'expert', pairs)]
    slice x0 -> x3, local copies, waits for them, and re-layouts: none -> 3.61 us  [the longest x1 3.08 us: layer(): first[:, :, model_width:]]
    another operation x0 -> x1, local copies, waits for them, and re-layouts: none -> 3.1 us  [layer(): extra = extra.reshape(experts * EXTRA, model_width)]
  transfers between devices with their start and end apart: 2 -> 5, of which waited for: 2 -> 3; matrix products, arithmetic and copies ran while one was open for 11% -> 15% of each run, Pallas kernels for 0% -> 7%
where the time goes in v2:
time: 237 us; the launch traced here: 235 us
  waiting for transfers between devices  143 us (60%)
  matrix products  27.1 us (11%)
  Pallas kernels  27 us (11%)
  starting transfers between devices  25.7 us (11%)
  local copies, waits for them, and re-layouts  8.96 us (4%)
    all_to_all x2, waiting for transfers between devices, exchange(): return lax.all_to_all(block, AXES, split_axis=0, concat_axis=0, tiled=True)  137 us
    all_to_all x2, starting transfers between devices, exchange(): return lax.all_to_all(block, AXES, split_axis=0, concat_axis=0, tiled=True)  19.6 us
    pallas_call x2, Pallas kernels, pack(): pl.pallas_call(kernel, grid=(experts // GROUP,), in_specs=[pl.BlockSpec(x...  18.2 us
    dot_general x1, matrix products, layer(): jnp.dot(inputs, gate_up[0, 0], preferred_element_type=jnp.float32)  12 us
    dot_general x1, matrix products, layer(): up_out = jnp.dot(inputs, gate_up[0, 1], preferred_element_type=jnp.float32)  11.6 us
    pallas_call x1, Pallas kernels, finish(): pl.pallas_call(finish_kernel, grid=(rows // block,), in_specs=[row_block(...  8.83 us
    ppermute x1, waiting for transfers between devices, layer(): lax.ppermute(jnp.where(own_marked, low[:, BASE + EXTRA:], extra_back), 'e...  6.22 us
  transfers between devices with their start and end apart: 5, of which 3 were waited for; matrix products, arithmetic and copies ran while one was open for 15% of the time, Pallas kernels for 7%

profile of v2, /device:TPU:5, one launch (start us, length us, event | category | flops | bytes accessed | tf_op | source)
XLA Modules:
  0.0 235.4 jit_solution(16776114031218529291)
XLA Ops:
  0.6 0.0 copy-start
  0.6 10.8 %shard_map.105 = bf16[128,8,5120]{2,1,0:T(8,128)(2,1)} custom-call(s32[4,128]{1,0:T(4,128)} %bitcast.52, f32[4,128]{1,0:T(4,128)} %bitcast.54, s32[1,128]{1,0:T(1,128)} %bitcast.58, s32[1,128]{1,0:T(1,128)} %bitcast.56, bf16[128,4096]{1,0:T(8,128)(2,1)} %tokens.1, bf16[128,4096]{1,0:T(8,128)(2,1)} %cotangent.3), custom_call_target="tpu_custom_call" | custom-call | tf_op jit(solution)/shard_map/pallas_call | solution.py:92
  11.5 11.2 %all-to-all-start.1 = ((bf16[128,8,5120]{2,1,0:T(8,128)(2,1)}), bf16[128,8,5120]{2,1,0:T(8,128)(2,1)}, u32[]{:S(2)}, u32[]{:S(2)}) async-start(bf16[128,8,5120]{2,1,0:T(8,128)(2,1)} %shard_map.105), calls=%async_computation.1 | async-start | bytes 20971520 | tf_op jit(solution)/shard_map/all_to_all | solution.py:151
  22.7 0.0 copy-start.5
  22.7 2.8 %collective-permute-start = (bf16[32,4096]{1,0:T(8,128)(2,1)S(1)}, bf16[32,4096]{1,0:T(8,128)(2,1)S(1)}, u32[]{:S(2)}, u32[]{:S(2)}) collective-permute-start(bf16[32,4096]{1,0:T(8,128)(2,1)S(1)} %bitcast.48), channel_id=1, source_target_pairs={{0,8},{1,9},{2,10},{3,11},{4,12},{5,13},{6,14},{7,15},{8,0},{9,1},... | collective-permute-start | bytes 786440 | tf_op jit(solution)/shard_map/ppermute | solution.py:166
  25.5 7.3 %shard_map.104 = bf16[128,8,2048]{2,1,0:T(8,128)(2,1)} custom-call(s32[4,128]{1,0:T(4,128)} %bitcast.53, f32[4,128]{1,0:T(4,128)} %bitcast.55, s32[1,128]{1,0:T(1,128)} %bitcast.59, s32[1,128]{1,0:T(1,128)} %bitcast.57, bf16[128,4096]{1,0:T(8,128)(2,1)} %cotangent.3), custom_call_target="tpu_custom_call" | custom-call | tf_op jit(solution)/shard_map/pallas_call | solution.py:92
  32.8 0.6 dynamic_slice.4
  34.1 128.6 %all-to-all-done.1 = bf16[128,8,5120]{2,1,0:T(8,128)(2,1)} async-done(((bf16[128,8,5120]{2,1,0:T(8,128)(2,1)}), bf16[128,8,5120]{2,1,0:T(8,128)(2,1)}, u32[]{:S(2)}, u32[]{:S(2)}) %all-to-all-start.1) | async-done | bytes 10485792 | tf_op jit(solution)/shard_map/all_to_all | solution.py:151
  162.7 8.5 %all-to-all-start = ((bf16[128,8,2048]{2,1,0:T(8,128)(2,1)}), bf16[128,8,2048]{2,1,0:T(8,128)(2,1)}, u32[]{:S(2)}, u32[]{:S(2)}) async-start(bf16[128,8,2048]{2,1,0:T(8,128)(2,1)} %shard_map.104), calls=%async_computation | async-start | bytes 8388608 | tf_op jit(solution)/shard_map/all_to_all | solution.py:151
  171.2 12.0 %fusion.1 = f32[1024,768]{1,0:T(8,128)} fusion(bf16[128,8,5120]{2,1,0:T(8,128)(2,1)} %all-to-all-done.1, bf16[1,2,4096,768]{3,2,1,0:T(8,128)(2,1)} %param.15), kind=kOutput, calls=%fused_computation.2 | convolution fusion | flops 6442450944 | bytes 17825792 | tf_op jit(solution)/shard_map/dot_general | solution.py:182
  183.2 3.1 %slice.29 = bf16[128,8,1024]{2,1,0:T(8,128)(2,1)} slice(bf16[128,8,5120]{2,1,0:T(8,128)(2,1)} %all-to-all-done.1), slice={[0:128], [0:8], [4096:5120]} | slice | bytes 4194304 | tf_op jit(solution)/shard_map/slice | solution.py:193
  186.3 3.1 %reshape_reshape.3 = bf16[256,4096]{1,0:T(8,128)(2,1)S(1)} reshape(bf16[128,8,1024]{2,1,0:T(8,128)(2,1)} %slice.29) | data formatting | bytes 4194304 | tf_op jit(solution)/shard_map/reshape;reshape | solution.py:194
  189.4 0.0 collective-permute-done
  189.4 0.7 fusion.11
  190.1 0.1 copy.18
  190.3 0.1 copy.21
  190.3 11.6 %multiply_convert_fusion.hidden = bf16[1024,768]{1,0:T(8,128)(2,1)S(1)} fusion(f32[1024,768]{1,0:T(8,128)} %fusion.1, bf16[1,2,4096,768]{3,2,1,0:T(8,128)(2,1)} %param.15, bf16[128,8,5120]{2,1,0:T(8,128)(2,1)} %all-to-all-done.1), kind=kOutput, calls=%fused_computation.7 | convolution fusion | flops 6447169536 | bytes 19398656 | tf_op jit(solution)/shard_map/dot_general | solution.py:183
  201.9 1.2 copy-done.1
  203.1 0.5 fusion.8.low
  203.6 0.1 fusion.23
  203.8 0.1 copy.26
  203.9 2.8 %collective-permute-start.1 = (bf16[128,2,32]{0,2,1:T(8,128)(2,1)S(1)}, bf16[128,2,32]{0,2,1:T(8,128)(2,1)S(1)}, u32[]{:S(2)}, u32[]{:S(2)}) collective-permute-start(bf16[128,2,32]{0,2,1:T(8,128)(2,1)S(1)} %broadcast_select_fusion.1), channel_id=1, source_target_pairs={{0,8},{1,9},{2,10},{3,11},{4,12},{5,13},{6,14},{7,15},{8,0},{9,1},... | collective-permute-start | bytes 49160 | tf_op jit(solution)/shard_map/ppermute | solution.py:200
  206.7 0.1 copy.28
  206.7 6.2 %collective-permute-done.1 = bf16[128,2,32]{0,2,1:T(8,128)(2,1)S(1)} collective-permute-done((bf16[128,2,32]{0,2,1:T(8,128)(2,1)S(1)}, bf16[128,2,32]{0,2,1:T(8,128)(2,1)S(1)}, u32[]{:S(2)}, u32[]{:S(2)}) %collective-permute-start.1) | collective-permute-done | bytes 16416 | tf_op jit(solution)/shard_map/ppermute | solution.py:200
  213.0 0.1 copy.24
  213.1 0.5 fusion.24
  213.6 0.5 collective-permute-start.2
  214.1 8.4 %all-to-all-done = bf16[128,8,2048]{2,1,0:T(8,128)(2,1)} async-done(((bf16[128,8,2048]{2,1,0:T(8,128)(2,1)}), bf16[128,8,2048]{2,1,0:T(8,128)(2,1)}, u32[]{:S(2)}, u32[]{:S(2)}) %all-to-all-start) | async-done | bytes 4194336 | tf_op jit(solution)/shard_map/all_to_all | solution.py:151
  222.4 8.8 %shard_map.106 = (f32[32,4096]{1,0:T(8,128)}, f32[32,768]{1,0:T(8,128)}) custom-call(bf16[1024,2048]{1,0:T(8,128)(2,1)} %bitcast.4.base, bf16[1024,32]{1,0:T(8,128)(2,1)} %copy-done.4, bf16[1024,768]{1,0:T(8,128)(2,1)} %copy-done.1, bf16[32,4096]{1,0:T(8,128)(2,1)} %bitcast.47), custom_call_target="tpu_custom_call" | custom-call | tf_op jit(solution)/shard_map/pallas_call | solution.py:138
  231.3 0.4 slice.31
  231.7 1.8 fusion.10
  233.5 1.9 add_bitcast_fusion
  (12 shorter events, 0.0 us)
Async XLA Ops:
  0.6 202.5 %copy-start = (bf16[1,32,768]{2,1,0:T(8,128)(2,1)S(1)}, bf16[1,32,768]{2,1,0:T(8,128)(2,1)}, u32[]{:S(2)}) copy-start(bf16[1,32,768]{2,1,0:T(8,128)(2,1)} %param.16) | copy-start | bytes 147460
  11.5 11.2 %copy-start.3 = (bf16[1,32,4096]{2,1,0:T(8,128)(2,1)S(1)}, bf16[1,32,4096]{2,1,0:T(8,128)(2,1)}, u32[]{:S(2)}) copy-start(bf16[1,32,4096]{2,1,0:T(8,128)(2,1)} %param.17) | copy-start | bytes 786436
  11.5 151.2 %all-to-all-start.1 = ((bf16[128,8,5120]{2,1,0:T(8,128)(2,1)}), bf16[128,8,5120]{2,1,0:T(8,128)(2,1)}, u32[]{:S(2)}, u32[]{:S(2)}) async-start(bf16[128,8,5120]{2,1,0:T(8,128)(2,1)} %shard_map.105), calls=%async_computation.1 | async-start | bytes 20971520 | tf_op jit(solution)/shard_map/all_to_all | solution.py:151
  22.7 10.2 %copy-start.5 = (s32[128]{0:T(128)S(1)}, s32[128]{0:T(128)}, u32[]{:S(2)}) copy-start(s32[128]{0:T(128)} %param.13) | copy-start | bytes 1540
  22.7 166.7 %collective-permute-start = (bf16[32,4096]{1,0:T(8,128)(2,1)S(1)}, bf16[32,4096]{1,0:T(8,128)(2,1)S(1)}, u32[]{:S(2)}, u32[]{:S(2)}) collective-permute-start(bf16[32,4096]{1,0:T(8,128)(2,1)S(1)} %bitcast.48), channel_id=1, source_target_pairs={{0,8},{1,9},{2,10},{3,11},{4,12},{5,13},{6,14},{7,15},{8,0},{9,1},... | collective-permute-start | bytes 786440 | tf_op jit(solution)/shard_map/ppermute | solution.py:166
  162.7 59.8 %all-to-all-start = ((bf16[128,8,2048]{2,1,0:T(8,128)(2,1)}), bf16[128,8,2048]{2,1,0:T(8,128)(2,1)}, u32[]{:S(2)}, u32[]{:S(2)}) async-start(bf16[128,8,2048]{2,1,0:T(8,128)(2,1)} %shard_map.104), calls=%async_computation | async-start | bytes 8388608 | tf_op jit(solution)/shard_map/all_to_all | solution.py:151
  201.9 1.2 copy-start.1
  203.6 18.8 %copy-start.4 = (bf16[1024,32]{1,0:T(8,128)(2,1)}, bf16[1024,32]{1,0:T(8,128)(2,1)S(1)}, u32[]{:S(2)}) copy-start(bf16[1024,32]{1,0:T(8,128)(2,1)S(1)} %fusion.8.low) | copy-start | bytes 196612
  203.9 9.1 %collective-permute-start.1 = (bf16[128,2,32]{0,2,1:T(8,128)(2,1)S(1)}, bf16[128,2,32]{0,2,1:T(8,128)(2,1)S(1)}, u32[]{:S(2)}, u32[]{:S(2)}) collective-permute-start(bf16[128,2,32]{0,2,1:T(8,128)(2,1)S(1)} %broadcast_select_fusion.1), channel_id=1, source_target_pairs={{0,8},{1,9},{2,10},{3,11},{4,12},{5,13},{6,14},{7,15},{8,0},{9,1},... | collective-permute-start | bytes 49160 | tf_op jit(solution)/shard_map/ppermute | solution.py:200
  213.6 19.9 %collective-permute-start.2 = (f32[32,4096]{1,0:T(8,128)S(1)}, f32[32,4096]{1,0:T(8,128)S(1)}, u32[]{:S(2)}, u32[]{:S(2)}) collective-permute-start(f32[32,4096]{1,0:T(8,128)S(1)} %fusion.24), channel_id=1, source_target_pairs={{0,8},{1,9},{2,10},{3,11},{4,12},{5,13},{6,14},{7,15},{8,0},{9,1},... | collective-permute-start | bytes 1572872 | tf_op jit(solution)/shard_map/ppermute | solution.py:210
  222.4 8.8 %copy-start.2 = (bf16[1024,768]{1,0:T(8,128)(2,1)S(1)}, bf16[1024,768]{1,0:T(8,128)(2,1)}, u32[]{:S(2)}) copy-start(bf16[1024,768]{1,0:T(8,128)(2,1)} %copy-done.1) | copy-start | bytes 4718596

commit v3 on v2

--- a/solution.py
+++ b/solution.py
@@ -59,92 +59,108 @@
     return (total.reshape(group, SLOTS, width) * factor).astype(jnp.bfloat16)
 
 
-def pack_first_kernel(half, room, routing, probs, marks, caps, tokens, cotangent, out):
+def pack_kernel(half, room, routing, probs, marks, caps, own, tokens, cotangent, first, second):
     tok_count, width = tokens.shape
     experts = block_experts()
     marked = look_up(marks[...], experts)
     limit = look_up(caps[...], experts) + room * marked
-    rank, _ = slot_table(experts, routing[...], probs[...], limit)
+    rank, weight = slot_table(experts, routing[...], probs[...], limit)
     sublane = lax.broadcasted_iota(jnp.int32, (GROUP, SLOTS, tok_count), 1)
     pick = jnp.where(rank[:, None, :] == sublane, 1.0, 0.0).astype(jnp.bfloat16)
     rows = jnp.dot(
         pick.reshape(GROUP * SLOTS, tok_count), tokens[...], preferred_element_type=jnp.float32
     )
-    out[:, :, :width] = rows.astype(jnp.bfloat16).reshape(GROUP, SLOTS, width)
+    first[:, :, :width] = rows.reshape(GROUP, SLOTS, width).astype(jnp.bfloat16)
     hot = jnp.where(marked == 1, experts, experts ^ half)
     hot_rank, hot_weight = slot_table(
         hot, routing[...], probs[...], look_up(caps[...], hot) + room
     )
     hot_rank = hot_rank - jnp.where(marked == 1, BASE, BASE + EXTRA)
-    out[:, :, width:] = spread(hot_rank, hot_weight, cotangent, SLOTS // EXTRA)
-
-
-def pack_second_kernel(room, routing, probs, marks, caps, cotangent, out):
-    experts = block_experts()
-    limit = look_up(caps[...], experts) + room * look_up(marks[...], experts)
-    rank, weight = slot_table(experts, routing[...], probs[...], limit)
-    out[...] = spread(rank, weight, cotangent, SLOTS // BASE)
-
-
-def pack(kernel, tables, arrays, width):
-    experts = tables[-1].shape[1]
+    first[:, :, width:] = spread(hot_rank, hot_weight, cotangent, SLOTS // EXTRA)
+    second[...] = spread(rank, weight, cotangent, SLOTS // BASE)
+
+
+def pack(half, room, tables, arrays):
+    experts = tables[2].shape[1]
+    model_width = arrays[0].shape[1]
     operands = tables + arrays
+    widths = (model_width + EXTRA * model_width // SLOTS, BASE * model_width // SLOTS)
     return pl.pallas_call(
-        kernel,
+        functools.partial(pack_kernel, half, room),
         grid=(experts // GROUP,),
         in_specs=[pl.BlockSpec(x.shape, lambda i: (0, 0)) for x in operands],
-        out_specs=pl.BlockSpec((GROUP, SLOTS, width), lambda i: (i, 0, 0)),
-        out_shape=jax.ShapeDtypeStruct((experts, SLOTS, width), jnp.bfloat16),
+        out_specs=[pl.BlockSpec((GROUP, SLOTS, w), lambda i: (i, 0, 0)) for w in widths],
+        out_shape=[jax.ShapeDtypeStruct((experts, SLOTS, w), jnp.bfloat16) for w in widths],
     )(*operands)
 
 
-def finish_kernel(base, low, hidden, own_out, grad, in_grad):
+def finish_kernel(base, low, hidden, wide_out, grad_start, in_start, grad, in_grad, total):
     step = pl.program_id(0)
     block, width = base.shape
-    parts = SLOTS // BASE
+    parts, rank_width = SLOTS // BASE, grad.shape[0]
     row = lax.broadcasted_iota(jnp.int32, (block, block), 0)
     column = lax.broadcasted_iota(jnp.int32, (block, block), 1)
     same = row // SLOTS == column // SLOTS
     widen = jnp.where(same & (row % SLOTS // parts == column % SLOTS), 1.0, 0.0).astype(low.dtype)
     narrow = jnp.where(same & (row % SLOTS * parts == column % SLOTS), 1.0, 0.0).astype(low.dtype)
-    rows_low = jnp.dot(widen, low[...], preferred_element_type=jnp.float32).astype(low.dtype)
+    rows_low = jnp.dot(
+        widen, jnp.tile(low[...], (1, parts)), preferred_element_type=jnp.float32
+    )
     part = lax.broadcasted_iota(jnp.int32, rows_low.shape, 0) % parts
-    back = None
-    for at in range(parts):
-        columns = slice(at * width, (at + 1) * width)
-        part_low = jnp.where(part == at, rows_low, jnp.zeros((), low.dtype))
-        new = lax.dot_general(
-            part_low, base[...], (((0,), (0,)), ((), ())), preferred_element_type=jnp.float32
-        )
-        grad[:, columns] = jnp.where(step == 0, 0.0, grad[:, columns]) + new
-        half_back = lax.dot_general(
-            base[...], own_out[:, columns], (((1,), (1,)), ((), ())), preferred_element_type=jnp.float32
-        )
-        back = half_back if back is None else back + pltpu.roll(half_back, block - at, 0)
+    own = part == lax.broadcasted_iota(jnp.int32, rows_low.shape, 1) // rank_width
+    wide_low = jnp.where(own, rows_low, 0.0).astype(low.dtype)
+    new = lax.dot_general(
+        wide_low, base[...], (((0,), (0,)), ((), ())), preferred_element_type=jnp.float32
+    )
+    halves = lax.dot_general(
+        base[...], wide_out[...], (((1,), (1,)), ((), ())), preferred_element_type=jnp.float32
+    )
+    back = halves[:, :rank_width]
+    for at in range(1, parts):
+        later = halves[:, at * rank_width : (at + 1) * rank_width]
+        back = back + pltpu.roll(later, block - at, 0)
     back = (SCALE * back).astype(jnp.bfloat16)
     back = jnp.dot(narrow, back, preferred_element_type=jnp.float32).astype(jnp.bfloat16)
     new_in = lax.dot_general(
         back, hidden[...], (((0,), (0,)), ((), ())), preferred_element_type=jnp.float32
     )
-    in_grad[...] = jnp.where(step == 0, 0.0, in_grad[...]) + new_in
-
-
-def finish(base, low, hidden, own_out):
+
+    @pl.when(step == 0)
+    def _():
+        total[...] = new
+        in_grad[...] = in_start[...] + new_in
+
+    @pl.when(step > 0)
+    def _():
+        total[...] += new
+        in_grad[...] += new_in
+
+    @pl.when(step == pl.num_programs(0) - 1)
+    def _():
+        for at in range(parts):
+            columns = slice(at * width, (at + 1) * width)
+            rows = slice(at * rank_width, (at + 1) * rank_width)
+            grad[:, columns] = grad_start[:, columns] + total[rows, :]
+
+
+def finish(base, low, hidden, wide_out, grad_start, in_start):
     rows, width = base.shape
     rank_width, hidden_width = low.shape[1], hidden.shape[1]
     block = rows // 4
     row_block = lambda columns: pl.BlockSpec((block, columns), lambda i: (i, 0))
-    kept = lambda shape: pl.BlockSpec(shape, lambda i: (0, 0))
+    kept = lambda array: pl.BlockSpec(array.shape, lambda i: (0, 0))
     return pl.pallas_call(
         finish_kernel,
         grid=(rows // block,),
-        in_specs=[row_block(width), row_block(rank_width), row_block(hidden_width), kept(own_out.shape)],
-        out_specs=[kept(own_out.shape), kept((rank_width, hidden_width))],
+        in_specs=[row_block(width), row_block(rank_width), row_block(hidden_width)]
+        + [kept(wide_out), kept(grad_start), kept(in_start)],
+        out_specs=[kept(grad_start), kept(in_start)],
         out_shape=[
-            jax.ShapeDtypeStruct(own_out.shape, jnp.float32),
-            jax.ShapeDtypeStruct((rank_width, hidden_width), jnp.float32),
+            jax.ShapeDtypeStruct(grad_start.shape, jnp.float32),
+            jax.ShapeDtypeStruct(in_start.shape, jnp.float32),
         ],
-    )(base, low, hidden, own_out)
+        scratch_shapes=[pltpu.VMEM((SLOTS // BASE * rank_width, width), jnp.float32)],
+    )(base, low, hidden, wide_out, grad_start, in_start)
 
 
 def exchange(block):
@@ -165,17 +181,15 @@
 
     partner_out = lax.ppermute(own_out, "expert", pairs)
     room = tokens.shape[0] * routing.shape[1] // experts
-    tables = (routing.T, router_probs.T, hot_marks[None, :], cap_counts[None, :])
-    first = pack(
-        functools.partial(pack_first_kernel, half, room),
-        tables,
-        (tokens, cotangent),
-        model_width + EXTRA * model_width // SLOTS,
-    )
+    tables = (
+        routing.T,
+        router_probs.T,
+        hot_marks[None, :],
+        cap_counts[None, :],
+        own_marked.astype(jnp.int32).reshape(1, 1),
+    )
+    first, second = pack(half, room, tables, (tokens, cotangent))
     first = exchange(first)
-    second = pack(
-        functools.partial(pack_second_kernel, room), tables, (cotangent,), BASE * model_width // SLOTS
-    )
     second = exchange(second)
 
     inputs = first[:, :, :model_width].reshape(experts * SLOTS, model_width)
@@ -214,14 +228,19 @@
         "sjr,sjf->rf", hot_back, hidden[:, BASE:], preferred_element_type=jnp.float32
     )
 
-    base_grad, base_in = finish(
-        second.reshape(experts * SLOTS, BASE * model_width // SLOTS),
+    parts, width = SLOTS // BASE, BASE * model_width // SLOTS
+    wide_out = jnp.concatenate(
+        [own_out[:, at * width : (at + 1) * width] for at in range(parts)], axis=0
+    )
+    grad, in_grad = finish(
+        second.reshape(experts * SLOTS, width),
         low.reshape(experts * SLOTS, rank_width),
         hidden.reshape(experts * SLOTS, hidden_width),
-        own_out,
-    )
-    in_grad = base_in + in_grad
-    out_grad = base_grad + jnp.where(own_marked, extra_grad + returned, 0.0)
+        wide_out,
+        jnp.where(own_marked, extra_grad, 0.0),
+        in_grad,
+    )
+    out_grad = grad + jnp.where(own_marked, returned, 0.0)
     return in_grad[None], out_grad[None]
 
 

time: 237 us -> 241 us (1.017); the launches traced: 235 us -> 236 us
  waiting for transfers between devices: 143 us -> 151 us
  Pallas kernels: 27 us -> 21.1 us
    all_to_all x2, waiting for transfers between devices: 137 us -> 143 us  [exchange(): return lax.all_to_all(block, AXES, split_axis=0, concat_axis=0, tiled=True)]
    pallas_call x2 -> x1, Pallas kernels: 18.2 us -> 12.7 us  [pack(): pl.pallas_call(functools.partial(pack_kernel, half, room), grid=(experts...]
  transfers between devices with their start and end apart: 5 -> 5, of which waited for: 3 -> 3; matrix products, arithmetic and copies ran while one was open for 15% -> 14% of each run, Pallas kernels for 7% -> 4%
where the time goes in v3:
time: 241 us; the launch traced here: 236 us
  waiting for transfers between devices  151 us (63%)
  starting transfers between devices  25.7 us (11%)
  matrix products  25.4 us (11%)
  Pallas kernels  21.1 us (9%)
  local copies, waits for them, and re-layouts  9.66 us (4%)
  other arithmetic  2.64 us (1%)
    all_to_all x2, waiting for transfers between devices, exchange(): return lax.all_to_all(block, AXES, split_axis=0, concat_axis=0, tiled=True)  143 us
    all_to_all x2, starting transfers between devices, exchange(): return lax.all_to_all(block, AXES, split_axis=0, concat_axis=0, tiled=True)  19.7 us
    pallas_call x1, Pallas kernels, pack(): pl.pallas_call(functools.partial(pack_kernel, half, room), grid=(experts...  12.7 us
    dot_general x1, matrix products, layer(): up_out = jnp.dot(inputs, gate_up[0, 1], preferred_element_type=jnp.float32)  11.1 us
    dot_general x1, matrix products, layer(): jnp.dot(inputs, gate_up[0, 0], preferred_element_type=jnp.float32)  10.9 us
    pallas_call x1, Pallas kernels, finish(): pl.pallas_call(finish_kernel, grid=(rows // block,), in_specs=[row_block(...  8.38 us
    ppermute x1, waiting for transfers between devices, layer(): lax.ppermute(jnp.where(own_marked, low[:, BASE + EXTRA:], extra_back), 'e...  7.79 us
  transfers between devices with their start and end apart: 5, of which 3 were waited for; matrix products, arithmetic and copies ran while one was open for 14% of the time, Pallas kernels for 4%

profile of v3, /device:TPU:5, one launch (start us, length us, event | category | flops | bytes accessed | tf_op | source)
XLA Modules:
  0.0 236.5 jit_solution(11132584609112535583)
XLA Ops:
  0.6 0.0 copy-start
  0.7 1.2 dynamic_slice.4
  2.5 12.7 %shard_map.104 = (bf16[128,8,5120]{2,1,0:T(8,128)(2,1)}, bf16[128,8,2048]{2,1,0:T(8,128)(2,1)}) custom-call(s32[4,128]{1,0:T(4,128)} %bitcast.48, f32[4,128]{1,0:T(4,128)} %bitcast.49, s32[1,128]{1,0:T(1,128)} %bitcast.50, s32[1,128]{1,0:T(1,128)} %bitcast.51, s32[1,1]{1,0:T(1,128)} %bitcast.4.own, bf16[128,4096]{1,0:T(8,128)(2,1)} %tokens.1, ...), custom_call_target="tpu_custom_call" | custom-call | tf_op jit(solution)/shard_map/pallas_call | solution.py:88
  15.3 11.2 %all-to-all-start.1 = ((bf16[128,8,5120]{2,1,0:T(8,128)(2,1)}), bf16[128,8,5120]{2,1,0:T(8,128)(2,1)}, u32[]{:S(2)}, u32[]{:S(2)}) async-start(bf16[128,8,5120]{2,1,0:T(8,128)(2,1)} %get-tuple-element.7), calls=%async_computation.1 | async-start | bytes 20971520 | tf_op jit(solution)/shard_map/all_to_all | solution.py:167
  26.5 2.8 %collective-permute-start = (bf16[32,4096]{1,0:T(8,128)(2,1)S(1)}, bf16[32,4096]{1,0:T(8,128)(2,1)S(1)}, u32[]{:S(2)}, u32[]{:S(2)}) collective-permute-start(bf16[32,4096]{1,0:T(8,128)(2,1)S(1)} %bitcast.43), channel_id=1, source_target_pairs={{0,8},{1,9},{2,10},{3,11},{4,12},{5,13},{6,14},{7,15},{8,0},{9,1},... | collective-permute-start | bytes 786440 | tf_op jit(solution)/shard_map/ppermute | solution.py:182
  29.2 137.2 %all-to-all-done.1 = bf16[128,8,5120]{2,1,0:T(8,128)(2,1)} async-done(((bf16[128,8,5120]{2,1,0:T(8,128)(2,1)}), bf16[128,8,5120]{2,1,0:T(8,128)(2,1)}, u32[]{:S(2)}, u32[]{:S(2)}) %all-to-all-start.1) | async-done | bytes 10485792 | tf_op jit(solution)/shard_map/all_to_all | solution.py:167
  166.5 8.5 %all-to-all-start = ((bf16[128,8,2048]{2,1,0:T(8,128)(2,1)}), bf16[128,8,2048]{2,1,0:T(8,128)(2,1)}, u32[]{:S(2)}, u32[]{:S(2)}) async-start(bf16[128,8,2048]{2,1,0:T(8,128)(2,1)} %get-tuple-element.6), calls=%async_computation | async-start | bytes 8388608 | tf_op jit(solution)/shard_map/all_to_all | solution.py:167
  174.9 10.9 %fusion.1 = f32[1024,768]{1,0:T(8,128)S(1)} fusion(bf16[128,8,5120]{2,1,0:T(8,128)(2,1)} %all-to-all-done.1, bf16[1,2,4096,768]{3,2,1,0:T(8,128)(2,1)} %param.15), kind=kOutput, calls=%fused_computation.2 | convolution fusion | flops 6442450944 | bytes 17825792 | tf_op jit(solution)/shard_map/dot_general | solution.py:196
  185.9 11.1 %multiply_convert_fusion.hidden = bf16[1024,768]{1,0:T(8,128)(2,1)S(1)} fusion(f32[1024,768]{1,0:T(8,128)S(1)} %fusion.1, bf16[1,2,4096,768]{3,2,1,0:T(8,128)(2,1)} %param.15, bf16[128,8,5120]{2,1,0:T(8,128)(2,1)} %all-to-all-done.1), kind=kOutput, calls=%fused_computation.7 | convolution fusion | flops 6447169536 | bytes 19398656 | tf_op jit(solution)/shard_map/dot_general | solution.py:197
  197.0 1.2 copy-done.1
  198.1 0.5 fusion.8.low
  198.7 0.1 fusion.21
  198.8 0.1 copy.27
  198.9 3.1 %slice.41 = bf16[128,8,1024]{2,1,0:T(8,128)(2,1)} slice(bf16[128,8,5120]{2,1,0:T(8,128)(2,1)} %all-to-all-done.1), slice={[0:128], [0:8], [4096:5120]} | slice | bytes 4194304 | tf_op jit(solution)/shard_map/slice | solution.py:207
  202.0 3.1 %reshape_reshape.3 = bf16[256,4096]{1,0:T(8,128)(2,1)S(1)} reshape(bf16[128,8,1024]{2,1,0:T(8,128)(2,1)} %slice.41) | data formatting | bytes 4194304 | tf_op jit(solution)/shard_map/reshape;reshape | solution.py:208
  205.1 0.0 collective-permute-done
  205.1 0.7 fusion.9
  205.9 0.1 copy.20
  206.0 0.1 copy.21
  206.1 2.8 %collective-permute-start.1 = (bf16[128,2,32]{0,2,1:T(8,128)(2,1)S(1)}, bf16[128,2,32]{0,2,1:T(8,128)(2,1)S(1)}, u32[]{:S(2)}, u32[]{:S(2)}) collective-permute-start(bf16[128,2,32]{0,2,1:T(8,128)(2,1)S(1)} %broadcast_select_fusion.2), channel_id=1, source_target_pairs={{0,8},{1,9},{2,10},{3,11},{4,12},{5,13},{6,14},{7,15},{8,0},{9,1},... | collective-permute-start | bytes 49160 | tf_op jit(solution)/shard_map/ppermute | solution.py:214
  208.9 0.1 copy.26
  209.0 7.8 %collective-permute-done.1 = bf16[128,2,32]{0,2,1:T(8,128)(2,1)S(1)} collective-permute-done((bf16[128,2,32]{0,2,1:T(8,128)(2,1)S(1)}, bf16[128,2,32]{0,2,1:T(8,128)(2,1)S(1)}, u32[]{:S(2)}, u32[]{:S(2)}) %collective-permute-start.1) | collective-permute-done | bytes 16416 | tf_op jit(solution)/shard_map/ppermute | solution.py:214
  216.8 0.1 copy.22
  216.9 1.3 broadcast_select_fusion
  218.2 0.4 collective-permute-start.2
  218.6 0.7 pad_maximum_fusion.wide_out
  219.4 0.4 slice.42
  219.8 0.9 convolution_bitcast_fusion.in_start
  220.6 5.6 %all-to-all-done = bf16[128,8,2048]{2,1,0:T(8,128)(2,1)} async-done(((bf16[128,8,2048]{2,1,0:T(8,128)(2,1)}), bf16[128,8,2048]{2,1,0:T(8,128)(2,1)}, u32[]{:S(2)}, u32[]{:S(2)}) %all-to-all-start) | async-done | bytes 4194336 | tf_op jit(solution)/shard_map/all_to_all | solution.py:167
  226.2 8.4 %shard_map.105 = (f32[32,4096]{1,0:T(8,128)}, f32[32,768]{1,0:T(8,128)}) custom-call(bf16[1024,2048]{1,0:T(8,128)(2,1)} %bitcast.5.base, bf16[1024,32]{1,0:T(8,128)(2,1)} %copy-done.4, bf16[1024,768]{1,0:T(8,128)(2,1)} %copy-done.1, bf16[64,2048]{1,0:T(8,128)(2,1)} %pad_maximum_fusion.wide_out, f32[32,4096]{1,0:T(8,128)} %get-tuple-element.14.grad_start, ...), custom_call_target="tpu_custom_call" | custom-call | tf_op jit(solution)/shard_map/pallas_call | solution.py:152
  234.6 0.0 collective-permute-done.2
  234.6 1.9 add_bitcast_fusion
  (11 shorter events, 0.1 us)
Async XLA Ops:
  0.6 197.5 %copy-start = (bf16[1,32,768]{2,1,0:T(8,128)(2,1)S(1)}, bf16[1,32,768]{2,1,0:T(8,128)(2,1)}, u32[]{:S(2)}) copy-start(bf16[1,32,768]{2,1,0:T(8,128)(2,1)} %param.16) | copy-start | bytes 147460
  15.3 11.2 %copy-start.3 = (bf16[1,32,4096]{2,1,0:T(8,128)(2,1)S(1)}, bf16[1,32,4096]{2,1,0:T(8,128)(2,1)}, u32[]{:S(2)}) copy-start(bf16[1,32,4096]{2,1,0:T(8,128)(2,1)} %param.17) | copy-start | bytes 786436
  15.3 151.2 %all-to-all-start.1 = ((bf16[128,8,5120]{2,1,0:T(8,128)(2,1)}), bf16[128,8,5120]{2,1,0:T(8,128)(2,1)}, u32[]{:S(2)}, u32[]{:S(2)}) async-start(bf16[128,8,5120]{2,1,0:T(8,128)(2,1)} %get-tuple-element.7), calls=%async_computation.1 | async-start | bytes 20971520 | tf_op jit(solution)/shard_map/all_to_all | solution.py:167
  26.5 178.7 %collective-permute-start = (bf16[32,4096]{1,0:T(8,128)(2,1)S(1)}, bf16[32,4096]{1,0:T(8,128)(2,1)S(1)}, u32[]{:S(2)}, u32[]{:S(2)}) collective-permute-start(bf16[32,4096]{1,0:T(8,128)(2,1)S(1)} %bitcast.43), channel_id=1, source_target_pairs={{0,8},{1,9},{2,10},{3,11},{4,12},{5,13},{6,14},{7,15},{8,0},{9,1},... | collective-permute-start | bytes 786440 | tf_op jit(solution)/shard_map/ppermute | solution.py:182
  166.5 59.8 %all-to-all-start = ((bf16[128,8,2048]{2,1,0:T(8,128)(2,1)}), bf16[128,8,2048]{2,1,0:T(8,128)(2,1)}, u32[]{:S(2)}, u32[]{:S(2)}) async-start(bf16[128,8,2048]{2,1,0:T(8,128)(2,1)} %get-tuple-element.6), calls=%async_computation | async-start | bytes 8388608 | tf_op jit(solution)/shard_map/all_to_all | solution.py:167
  197.0 1.2 copy-start.1
  198.7 6.4 %copy-start.4 = (bf16[1024,32]{1,0:T(8,128)(2,1)}, bf16[1024,32]{1,0:T(8,128)(2,1)S(1)}, u32[]{:S(2)}) copy-start(bf16[1024,32]{1,0:T(8,128)(2,1)S(1)} %fusion.8.low) | copy-start | bytes 196612
  206.1 10.7 %collective-permute-start.1 = (bf16[128,2,32]{0,2,1:T(8,128)(2,1)S(1)}, bf16[128,2,32]{0,2,1:T(8,128)(2,1)S(1)}, u32[]{:S(2)}, u32[]{:S(2)}) collective-permute-start(bf16[128,2,32]{0,2,1:T(8,128)(2,1)S(1)} %broadcast_select_fusion.2), channel_id=1, source_target_pairs={{0,8},{1,9},{2,10},{3,11},{4,12},{5,13},{6,14},{7,15},{8,0},{9,1},... | collective-permute-start | bytes 49160 | tf_op jit(solution)/shard_map/ppermute | solution.py:214
  216.9 2.5 %copy-start.2 = (bf16[1024,768]{1,0:T(8,128)(2,1)S(1)}, bf16[1024,768]{1,0:T(8,128)(2,1)}, u32[]{:S(2)}) copy-start(bf16[1024,768]{1,0:T(8,128)(2,1)} %copy-done.1) | copy-start | bytes 4718596
  218.2 16.4 %collective-permute-start.2 = (f32[32,4096]{1,0:T(8,128)S(1)}, f32[32,4096]{1,0:T(8,128)S(1)}, u32[]{:S(2)}, u32[]{:S(2)}) collective-permute-start(f32[32,4096]{1,0:T(8,128)S(1)} %get-tuple-element.15), channel_id=1, source_target_pairs={{0,8},{1,9},{2,10},{3,11},{4,12},{5,13},{6,14},{7,15},{8,0},{9,1},... | collective-permute-start | bytes 1572872 | tf_op jit(solution)/shard_map/ppermute | solution.py:224

commit v4 on v3

--- a/solution.py
+++ b/solution.py
@@ -12,7 +12,8 @@
 SLOTS = 8
 BASE = 4
 EXTRA = 2
-GROUP = 16
+GROUP = 32
+CHUNK = 512
 AXES = ("dp", "expert")
 
 
@@ -42,24 +43,29 @@
     return first + lax.broadcasted_iota(jnp.int32, (GROUP, 1), 0)
 
 
-def spread(rank, weight, rows, parts):
+def spread(rank, weight, rows, count):
     group, tok_count = rank.shape
+    parts = SLOTS // count
     sublane = lax.broadcasted_iota(jnp.int32, (group, SLOTS, tok_count), 1)
     match = rank[:, None, :] == sublane // parts
     factor = jnp.sum(jnp.where(match, weight[:, None, :], 0.0), axis=2, keepdims=True)
     width = rows.shape[1] // parts
-    total = jnp.zeros((group * SLOTS, width), jnp.float32)
-    for part in range(parts):
-        pick = jnp.where(match & (sublane % parts == part), 1.0, 0.0).astype(jnp.bfloat16)
-        total += jnp.dot(
-            pick.reshape(group * SLOTS, tok_count),
-            rows[:, part * width : (part + 1) * width],
-            preferred_element_type=jnp.float32,
-        )
-    return (total.reshape(group, SLOTS, width) * factor).astype(jnp.bfloat16)
-
-
-def pack_kernel(half, room, routing, probs, marks, caps, own, tokens, cotangent, first, second):
+    picks = [
+        jnp.where(match & (sublane % parts == part), 1.0, 0.0).astype(jnp.bfloat16)
+        for part in range(parts)
+    ]
+    stacked = [rows[:, part * width : (part + 1) * width] for part in range(parts)]
+    picked = jnp.dot(
+        jnp.concatenate(picks, axis=2).reshape(group * SLOTS, parts * tok_count),
+        jnp.concatenate(stacked, axis=0),
+        preferred_element_type=jnp.float32,
+    )
+    return (picked.reshape(group, SLOTS, width) * factor).astype(jnp.bfloat16)
+
+
+def pack_kernel(
+    half, room, routing, probs, marks, caps, own, tokens, cotangent, first, second
+):
     tok_count, width = tokens.shape
     experts = block_experts()
     marked = look_up(marks[...], experts)
@@ -76,8 +82,8 @@
         hot, routing[...], probs[...], look_up(caps[...], hot) + room
     )
     hot_rank = hot_rank - jnp.where(marked == 1, BASE, BASE + EXTRA)
-    first[:, :, width:] = spread(hot_rank, hot_weight, cotangent, SLOTS // EXTRA)
-    second[...] = spread(rank, weight, cotangent, SLOTS // BASE)
+    first[:, :, width:] = spread(hot_rank, hot_weight, cotangent, EXTRA)
+    second[...] = spread(rank, weight, cotangent, BASE)
 
 
 def pack(half, room, tables, arrays):
@@ -94,24 +100,65 @@
     )(*operands)
 
 
-def finish_kernel(base, low, hidden, wide_out, grad_start, in_start, grad, in_grad, total):
+def choose(rows, columns, per_row, wanted):
+    row = lax.broadcasted_iota(jnp.int32, (rows, columns), 0)
+    column = lax.broadcasted_iota(jnp.int32, (rows, columns), 1)
+    same = row // per_row == column // SLOTS
+    hit = same & wanted(row % per_row, column % SLOTS)
+    return jnp.where(hit, 1.0, 0.0).astype(jnp.bfloat16)
+
+
+def prepare_kernel(low, hidden, wide_low, wide_hidden, own_low, own_hidden, far_low, far_hidden):
+    block, rank_width = low.shape
+    parts = SLOTS // BASE
+
+    def take(matrix, array):
+        return jnp.dot(matrix, array, preferred_element_type=jnp.float32)
+
+    widen = choose(block, block, SLOTS, lambda i, m: i // parts == m)
+    wide_hidden[...] = take(widen, hidden[...]).astype(jnp.bfloat16)
+    rows_low = take(widen, jnp.tile(low[...], (1, parts)))
+    part = lax.broadcasted_iota(jnp.int32, rows_low.shape, 0) % parts
+    own = part == lax.broadcasted_iota(jnp.int32, rows_low.shape, 1) // rank_width
+    wide_low[...] = jnp.where(own, rows_low, 0.0).astype(jnp.bfloat16)
+    extra = own_low.shape[0]
+    near = choose(extra, block, EXTRA, lambda i, m: i + BASE == m)
+    own_low[...] = take(near, low[...]).astype(jnp.bfloat16)
+    own_hidden[...] = take(near, hidden[...]).astype(jnp.bfloat16)
+    far = choose(extra, block, EXTRA, lambda i, m: i + BASE + EXTRA == m)
+    far_low[...] = take(far, low[...]).astype(jnp.bfloat16)
+    far_hidden[...] = take(far, hidden[...]).astype(jnp.bfloat16)
+
+
+def prepare(low, hidden):
+    rows, rank_width = low.shape
+    hidden_width = hidden.shape[1]
+    block, extra = rows // 4, rows * EXTRA // SLOTS
+    spec = lambda shape: pl.BlockSpec((shape[0] // 4, shape[1]), lambda i: (i, 0))
+    shapes = [(rows, SLOTS // BASE * rank_width), (rows, hidden_width)]
+    shapes += [(extra, rank_width), (extra, hidden_width)] * 2
+    return pl.pallas_call(
+        prepare_kernel,
+        grid=(rows // block,),
+        in_specs=[spec(low.shape), spec(hidden.shape)],
+        out_specs=[spec(shape) for shape in shapes],
+        out_shape=[jax.ShapeDtypeStruct(shape, jnp.bfloat16) for shape in shapes],
+    )(low, hidden)
+
+
+def finish_kernel(base, wide_low, wide_hidden, wide_out, grad_start, in_start, grad, in_grad, total):
     step = pl.program_id(0)
     block, width = base.shape
     parts, rank_width = SLOTS // BASE, grad.shape[0]
-    row = lax.broadcasted_iota(jnp.int32, (block, block), 0)
-    column = lax.broadcasted_iota(jnp.int32, (block, block), 1)
-    same = row // SLOTS == column // SLOTS
-    widen = jnp.where(same & (row % SLOTS // parts == column % SLOTS), 1.0, 0.0).astype(low.dtype)
-    narrow = jnp.where(same & (row % SLOTS * parts == column % SLOTS), 1.0, 0.0).astype(low.dtype)
-    rows_low = jnp.dot(
-        widen, jnp.tile(low[...], (1, parts)), preferred_element_type=jnp.float32
-    )
-    part = lax.broadcasted_iota(jnp.int32, rows_low.shape, 0) % parts
-    own = part == lax.broadcasted_iota(jnp.int32, rows_low.shape, 1) // rank_width
-    wide_low = jnp.where(own, rows_low, 0.0).astype(low.dtype)
-    new = lax.dot_general(
-        wide_low, base[...], (((0,), (0,)), ((), ())), preferred_element_type=jnp.float32
-    )
+    for start in range(0, width, CHUNK):
+        columns = slice(start, start + CHUNK)
+        new = lax.dot_general(
+            wide_low[...],
+            base[:, columns],
+            (((0,), (0,)), ((), ())),
+            preferred_element_type=jnp.float32,
+        )
+        total[:, columns] = new + jnp.where(step == 0, 0.0, total[:, columns])
     halves = lax.dot_general(
         base[...], wide_out[...], (((1,), (1,)), ((), ())), preferred_element_type=jnp.float32
     )
@@ -119,21 +166,13 @@
     for at in range(1, parts):
         later = halves[:, at * rank_width : (at + 1) * rank_width]
         back = back + pltpu.roll(later, block - at, 0)
-    back = (SCALE * back).astype(jnp.bfloat16)
-    back = jnp.dot(narrow, back, preferred_element_type=jnp.float32).astype(jnp.bfloat16)
+    whole = lax.broadcasted_iota(jnp.int32, back.shape, 0) % parts == 0
+    back = jnp.where(whole, SCALE * back, 0.0).astype(jnp.bfloat16)
     new_in = lax.dot_general(
-        back, hidden[...], (((0,), (0,)), ((), ())), preferred_element_type=jnp.float32
-    )
-
-    @pl.when(step == 0)
-    def _():
-        total[...] = new
-        in_grad[...] = in_start[...] + new_in
-
-    @pl.when(step > 0)
-    def _():
-        total[...] += new
-        in_grad[...] += new_in
+        back, wide_hidden[...], (((0,), (0,)), ((), ())), preferred_element_type=jnp.float32
+    )
+
+    in_grad[...] = new_in + jnp.where(step == 0, in_start[...], in_grad[...])
 
     @pl.when(step == pl.num_programs(0) - 1)
     def _():
@@ -143,24 +182,23 @@
             grad[:, columns] = grad_start[:, columns] + total[rows, :]
 
 
-def finish(base, low, hidden, wide_out, grad_start, in_start):
+def finish(base, wide_low, wide_hidden, wide_out, grad_start, in_start):
     rows, width = base.shape
-    rank_width, hidden_width = low.shape[1], hidden.shape[1]
-    block = rows // 4
-    row_block = lambda columns: pl.BlockSpec((block, columns), lambda i: (i, 0))
+    block = rows // 2
+    row_block = lambda array: pl.BlockSpec((block, array.shape[1]), lambda i: (i, 0))
     kept = lambda array: pl.BlockSpec(array.shape, lambda i: (0, 0))
     return pl.pallas_call(
         finish_kernel,
         grid=(rows // block,),
-        in_specs=[row_block(width), row_block(rank_width), row_block(hidden_width)]
+        in_specs=[row_block(base), row_block(wide_low), row_block(wide_hidden)]
         + [kept(wide_out), kept(grad_start), kept(in_start)],
         out_specs=[kept(grad_start), kept(in_start)],
         out_shape=[
             jax.ShapeDtypeStruct(grad_start.shape, jnp.float32),
             jax.ShapeDtypeStruct(in_start.shape, jnp.float32),
         ],
-        scratch_shapes=[pltpu.VMEM((SLOTS // BASE * rank_width, width), jnp.float32)],
-    )(base, low, hidden, wide_out, grad_start, in_start)
+        scratch_shapes=[pltpu.VMEM((wide_out.shape[0], width), jnp.float32)],
+    )(base, wide_low, wide_hidden, wide_out, grad_start, in_start)
 
 
 def exchange(block):
@@ -199,9 +237,7 @@
     low = (
         SCALE * jnp.einsum("nf,rf->nr", hidden, own_in, preferred_element_type=jnp.float32)
     ).astype(jnp.bfloat16)
-    rank_width, hidden_width = own_in.shape
-    hidden = hidden.reshape(experts, SLOTS, hidden_width)
-    low = low.reshape(experts, SLOTS, rank_width)
+    wide_low, wide_hidden, own_low, own_hidden, far_low, far_hidden = prepare(low, hidden)
 
     parts = SLOTS // EXTRA
     extra = first[:, :, model_width:].reshape(experts, EXTRA, parts, model_width // parts)
@@ -210,23 +246,12 @@
     extra_back = (
         SCALE * jnp.einsum("nd,rd->nr", extra, work_out, preferred_element_type=jnp.float32)
     ).astype(jnp.bfloat16)
-    extra_back = extra_back.reshape(experts, EXTRA, rank_width)
-    swapped = lax.ppermute(
-        jnp.where(own_marked, low[:, BASE + EXTRA :], extra_back), "expert", pairs
-    )
-    extra_low = jnp.where(own_marked, low[:, BASE : BASE + EXTRA], swapped)
-    extra_grad = jnp.einsum(
-        "nr,nd->rd",
-        extra_low.reshape(experts * EXTRA, rank_width),
-        extra,
-        preferred_element_type=jnp.float32,
-    )
+    swapped = lax.ppermute(jnp.where(own_marked, far_low, extra_back), "expert", pairs)
+    extra_low = jnp.where(own_marked, own_low, swapped)
+    extra_grad = jnp.einsum("nr,nd->rd", extra_low, extra, preferred_element_type=jnp.float32)
     returned = lax.ppermute(extra_grad, "expert", pairs)
-    hot_back = jnp.concatenate([extra_back, swapped], axis=1)
-    hot_back = jnp.where(own_marked, hot_back, jnp.zeros((), jnp.bfloat16))
-    in_grad = jnp.einsum(
-        "sjr,sjf->rf", hot_back, hidden[:, BASE:], preferred_element_type=jnp.float32
-    )
+    in_start = jnp.einsum("nr,nf->rf", extra_back, own_hidden, preferred_element_type=jnp.float32)
+    in_start += jnp.einsum("nr,nf->rf", swapped, far_hidden, preferred_element_type=jnp.float32)
 
     parts, width = SLOTS // BASE, BASE * model_width // SLOTS
     wide_out = jnp.concatenate(
@@ -234,11 +259,11 @@
     )
     grad, in_grad = finish(
         second.reshape(experts * SLOTS, width),
-        low.reshape(experts * SLOTS, rank_width),
-        hidden.reshape(experts * SLOTS, hidden_width),
+        wide_low,
+        wide_hidden,
         wide_out,
         jnp.where(own_marked, extra_grad, 0.0),
-        in_grad,
+        jnp.where(own_marked, in_start, 0.0),
     )
     out_grad = grad + jnp.where(own_marked, returned, 0.0)
     return in_grad[None], out_grad[None]

time: 241 us -> 240 us (level)
  waiting for transfers between devices: 151 us -> 154 us
    ppermute x1, waiting for transfers between devices: 0.01 us -> 5.92 us  [layer(): returned = lax.ppermute(extra_grad, 'expert', pairs)]
    all_to_all x2, waiting for transfers between devices: 143 us -> 137 us  [exchange(): return lax.all_to_all(block, AXES, split_axis=0, concat_axis=0, tiled=True)]
    pallas_call x0 -> x1, Pallas kernels: none -> 4.39 us  [prepare(): pl.pallas_call(prepare_kernel, grid=(rows // block,), in_specs=[spec(low....]
    ppermute x1, waiting for transfers between devices: 7.79 us -> 11.3 us  [layer(): lax.ppermute(jnp.where(own_marked, far_low, extra_back), 'expert', pairs)]
    pallas_call x1, Pallas kernels: 12.7 us -> 9.44 us  [pack(): pl.pallas_call(functools.partial(pack_kernel, half, room), grid=(experts...]
where the time goes in v4:
time: 240 us; the launch traced here: 238 us
  waiting for transfers between devices  154 us (64%)
  matrix products  26.3 us (11%)
  starting transfers between devices  25.6 us (11%)
  Pallas kernels  19.8 us (8%)
  local copies, waits for them, and re-layouts  7.48 us (3%)
  other arithmetic  2.61 us (1%)
    all_to_all x2, waiting for transfers between devices, exchange(): return lax.all_to_all(block, AXES, split_axis=0, concat_axis=0, tiled=True)  137 us
    all_to_all x2, starting transfers between devices, exchange(): return lax.all_to_all(block, AXES, split_axis=0, concat_axis=0, tiled=True)  19.6 us
    ppermute x1, waiting for transfers between devices, layer(): lax.ppermute(jnp.where(own_marked, far_low, extra_back), 'expert', pairs)  11.3 us
    dot_general x1, matrix products, layer(): up_out = jnp.dot(inputs, gate_up[0, 1], preferred_element_type=jnp.float32)  11.1 us
    dot_general x1, matrix products, layer(): jnp.dot(inputs, gate_up[0, 0], preferred_element_type=jnp.float32)  10.9 us
    pallas_call x1, Pallas kernels, pack(): pl.pallas_call(functools.partial(pack_kernel, half, room), grid=(experts...  9.44 us
    pallas_call x1, Pallas kernels, finish(): pl.pallas_call(finish_kernel, grid=(rows // block,), in_specs=[row_block(...  6 us
    ppermute x1, waiting for transfers between devices, layer(): returned = lax.ppermute(extra_grad, 'expert', pairs)  5.92 us
  transfers between devices with their start and end apart: 5, of which 3 were waited for; matrix products, arithmetic and copies ran while one was open for 14% of the time, Pallas kernels for 4%

profile of v4, /device:TPU:5, one launch (start us, length us, event | category | flops | bytes accessed | tf_op | source)
XLA Modules:
  0.0 237.7 jit_solution(17733652261149375322)
XLA Ops:
  0.6 0.0 copy-start
  0.7 1.2 dynamic_slice.4
  2.5 9.4 %shard_map.104 = (bf16[128,8,5120]{2,1,0:T(8,128)(2,1)}, bf16[128,8,2048]{2,1,0:T(8,128)(2,1)}) custom-call(s32[4,128]{1,0:T(4,128)} %bitcast.43, f32[4,128]{1,0:T(4,128)} %bitcast.44, s32[1,128]{1,0:T(1,128)} %bitcast.45, s32[1,128]{1,0:T(1,128)} %bitcast.46, s32[1,1]{1,0:T(1,128)} %bitcast.4.own, bf16[128,4096]{1,0:T(8,128)(2,1)} %tokens.1, ...), custom_call_target="tpu_custom_call" | custom-call | tf_op jit(solution)/shard_map/pallas_call | solution.py:94
  12.0 11.2 %all-to-all-start.1 = ((bf16[128,8,5120]{2,1,0:T(8,128)(2,1)}), bf16[128,8,5120]{2,1,0:T(8,128)(2,1)}, u32[]{:S(2)}, u32[]{:S(2)}) async-start(bf16[128,8,5120]{2,1,0:T(8,128)(2,1)} %get-tuple-element.13), calls=%async_computation.1 | async-start | bytes 20971520 | tf_op jit(solution)/shard_map/all_to_all | solution.py:205
  23.2 0.0 copy-done.4
  23.2 2.8 %collective-permute-start = (bf16[32,4096]{1,0:T(8,128)(2,1)S(1)}, bf16[32,4096]{1,0:T(8,128)(2,1)S(1)}, u32[]{:S(2)}, u32[]{:S(2)}) collective-permute-start(bf16[32,4096]{1,0:T(8,128)(2,1)S(1)} %bitcast.41), channel_id=1, source_target_pairs={{0,8},{1,9},{2,10},{3,11},{4,12},{5,13},{6,14},{7,15},{8,0},{9,1},... | collective-permute-start | bytes 786440 | tf_op jit(solution)/shard_map/ppermute | solution.py:220
  26.0 137.2 %all-to-all-done.1 = bf16[128,8,5120]{2,1,0:T(8,128)(2,1)} async-done(((bf16[128,8,5120]{2,1,0:T(8,128)(2,1)}), bf16[128,8,5120]{2,1,0:T(8,128)(2,1)}, u32[]{:S(2)}, u32[]{:S(2)}) %all-to-all-start.1) | async-done | bytes 10485792 | tf_op jit(solution)/shard_map/all_to_all | solution.py:205
  163.2 8.5 %all-to-all-start = ((bf16[128,8,2048]{2,1,0:T(8,128)(2,1)}), bf16[128,8,2048]{2,1,0:T(8,128)(2,1)}, u32[]{:S(2)}, u32[]{:S(2)}) async-start(bf16[128,8,2048]{2,1,0:T(8,128)(2,1)} %get-tuple-element.12), calls=%async_computation | async-start | bytes 8388608 | tf_op jit(solution)/shard_map/all_to_all | solution.py:205
  171.7 10.9 %fusion.1 = f32[1024,768]{1,0:T(8,128)S(1)} fusion(bf16[128,8,5120]{2,1,0:T(8,128)(2,1)} %all-to-all-done.1, bf16[1,2,4096,768]{3,2,1,0:T(8,128)(2,1)} %param.15), kind=kOutput, calls=%fused_computation.2 | convolution fusion | flops 6442450944 | bytes 17825792 | tf_op jit(solution)/shard_map/dot_general | solution.py:234
  182.6 11.1 %multiply_convert_fusion.hidden = bf16[1024,768]{1,0:T(8,128)(2,1)S(1)} fusion(f32[1024,768]{1,0:T(8,128)S(1)} %fusion.1, bf16[1,2,4096,768]{3,2,1,0:T(8,128)(2,1)} %param.15, bf16[128,8,5120]{2,1,0:T(8,128)(2,1)} %all-to-all-done.1), kind=kOutput, calls=%fused_computation.7 | convolution fusion | flops 6447169536 | bytes 19398656 | tf_op jit(solution)/shard_map/dot_general | solution.py:235
  193.7 0.0 copy-done
  193.7 0.0 copy-start.1
  193.7 1.3 fusion.8.low
  195.0 0.0 copy-done.1
  195.0 4.4 %shard_map.105 = (bf16[1024,64]{1,0:T(8,128)(2,1)}, bf16[1024,768]{1,0:T(8,128)(2,1)}, bf16[256,32]{1,0:T(8,128)(2,1)}, bf16[256,768]{1,0:T(8,128)(2,1)}, bf16[2...) custom-call(bf16[1024,32]{1,0:T(8,128)(2,1)} %fusion.8.low, bf16[1024,768]{1,0:T(8,128)(2,1)} %copy-done.1), custom_call_target="tpu_custom_call" | custom-call | tf_op jit(solution)/shard_map/pallas_call | solution.py:140
  199.4 3.1 %slice.27 = bf16[128,8,1024]{2,1,0:T(8,128)(2,1)} slice(bf16[128,8,5120]{2,1,0:T(8,128)(2,1)} %all-to-all-done.1), slice={[0:128], [0:8], [4096:5120]} | slice | bytes 4194304 | tf_op jit(solution)/shard_map/slice | solution.py:243
  202.4 3.1 %reshape_reshape.3 = bf16[256,4096]{1,0:T(8,128)(2,1)S(1)} reshape(bf16[128,8,1024]{2,1,0:T(8,128)(2,1)} %slice.27) | data formatting | bytes 4194304 | tf_op jit(solution)/shard_map/reshape;reshape | solution.py:244
  205.6 0.0 collective-permute-done
  205.6 0.7 broadcast_select_fusion.1
  206.3 2.8 %collective-permute-start.1 = (bf16[256,32]{1,0:T(8,128)(2,1)S(1)}, bf16[256,32]{1,0:T(8,128)(2,1)S(1)}, u32[]{:S(2)}, u32[]{:S(2)}) collective-permute-start(bf16[256,32]{1,0:T(8,128)(2,1)S(1)} %get-tuple-element.24), channel_id=1, source_target_pairs={{0,8},{1,9},{2,10},{3,11},{4,12},{5,13},{6,14},{7,15},{8,0},{9,1},... | collective-permute-start | bytes 49160 | tf_op jit(solution)/shard_map/ppermute | solution.py:249
  209.1 11.3 %collective-permute-done.1 = bf16[256,32]{1,0:T(8,128)(2,1)S(1)} collective-permute-done((bf16[256,32]{1,0:T(8,128)(2,1)S(1)}, bf16[256,32]{1,0:T(8,128)(2,1)S(1)}, u32[]{:S(2)}, u32[]{:S(2)}) %collective-permute-start.1) | collective-permute-done | bytes 16416 | tf_op jit(solution)/shard_map/ppermute | solution.py:249
  220.4 1.3 broadcast_select_fusion
  221.7 0.4 collective-permute-start.2
  222.1 0.7 pad_maximum_fusion.wide_out
  222.8 0.0 copy-done.3
  222.8 0.2 fusion.19
  223.0 0.0 copy-done.2
  223.0 0.9 fusion.10.in_start
  223.9 0.0 all-to-all-done
  223.9 6.0 %shard_map.106 = (f32[32,4096]{1,0:T(8,128)}, f32[32,768]{1,0:T(8,128)}) custom-call(bf16[1024,2048]{1,0:T(8,128)(2,1)} %bitcast.5.base, bf16[1024,64]{1,0:T(8,128)(2,1)} %get-tuple-element.14.wide_low, bf16[1024,768]{1,0:T(8,128)(2,1)} %get-tuple-element.15.wide_hidden, bf16[64,2048]{1,0:T(8,128)(2,1)} %pad_maximum_fusion.wide_out, ...), custom_call_target="tpu_custom_call" | custom-call | tf_op jit(solution)/shard_map/pallas_call | solution.py:190
  229.9 5.9 %collective-permute-done.2 = f32[32,4096]{1,0:T(8,128)S(1)} collective-permute-done((f32[32,4096]{1,0:T(8,128)S(1)}, f32[32,4096]{1,0:T(8,128)S(1)}, u32[]{:S(2)}, u32[]{:S(2)}) %collective-permute-start.2) | collective-permute-done | bytes 524320 | tf_op jit(solution)/shard_map/ppermute | solution.py:252
  235.8 1.9 add_bitcast_fusion
  (8 shorter events, 0.0 us)
Async XLA Ops:
  0.6 193.1 %copy-start = (bf16[1,32,768]{2,1,0:T(8,128)(2,1)S(1)}, bf16[1,32,768]{2,1,0:T(8,128)(2,1)}, u32[]{:S(2)}) copy-start(bf16[1,32,768]{2,1,0:T(8,128)(2,1)} %param.16) | copy-start | bytes 147460
  12.0 11.2 %copy-start.4 = (bf16[1,32,4096]{2,1,0:T(8,128)(2,1)S(1)}, bf16[1,32,4096]{2,1,0:T(8,128)(2,1)}, u32[]{:S(2)}) copy-start(bf16[1,32,4096]{2,1,0:T(8,128)(2,1)} %param.17) | copy-start | bytes 786436
  12.0 151.2 %all-to-all-start.1 = ((bf16[128,8,5120]{2,1,0:T(8,128)(2,1)}), bf16[128,8,5120]{2,1,0:T(8,128)(2,1)}, u32[]{:S(2)}, u32[]{:S(2)}) async-start(bf16[128,8,5120]{2,1,0:T(8,128)(2,1)} %get-tuple-element.13), calls=%async_computation.1 | async-start | bytes 20971520 | tf_op jit(solution)/shard_map/all_to_all | solution.py:205
  23.2 182.4 %collective-permute-start = (bf16[32,4096]{1,0:T(8,128)(2,1)S(1)}, bf16[32,4096]{1,0:T(8,128)(2,1)S(1)}, u32[]{:S(2)}, u32[]{:S(2)}) collective-permute-start(bf16[32,4096]{1,0:T(8,128)(2,1)S(1)} %bitcast.41), channel_id=1, source_target_pairs={{0,8},{1,9},{2,10},{3,11},{4,12},{5,13},{6,14},{7,15},{8,0},{9,1},... | collective-permute-start | bytes 786440 | tf_op jit(solution)/shard_map/ppermute | solution.py:220
  163.2 60.7 %all-to-all-start = ((bf16[128,8,2048]{2,1,0:T(8,128)(2,1)}), bf16[128,8,2048]{2,1,0:T(8,128)(2,1)}, u32[]{:S(2)}, u32[]{:S(2)}) async-start(bf16[128,8,2048]{2,1,0:T(8,128)(2,1)} %get-tuple-element.12), calls=%async_computation | async-start | bytes 8388608 | tf_op jit(solution)/shard_map/all_to_all | solution.py:205
  193.7 1.3 copy-start.1
  202.4 3.2 %copy-start.6 = (bf16[256,32]{1,0:T(8,128)(2,1)S(1)}, bf16[256,32]{1,0:T(8,128)(2,1)}, u32[]{:S(2)}) copy-start(bf16[256,32]{1,0:T(8,128)(2,1)} %get-tuple-element.17) | copy-start | bytes 49156
  202.4 18.0 %copy-start.5 = (bf16[256,32]{1,0:T(8,128)(2,1)S(1)}, bf16[256,32]{1,0:T(8,128)(2,1)}, u32[]{:S(2)}) copy-start(bf16[256,32]{1,0:T(8,128)(2,1)} %get-tuple-element.16) | copy-start | bytes 49156
  205.6 17.2 %copy-start.3 = (bf16[256,768]{1,0:T(8,128)(2,1)S(1)}, bf16[256,768]{1,0:T(8,128)(2,1)}, u32[]{:S(2)}) copy-start(bf16[256,768]{1,0:T(8,128)(2,1)} %get-tuple-element.18) | copy-start | bytes 1179652
  206.3 16.7 %copy-start.2 = (bf16[256,768]{1,0:T(8,128)(2,1)S(1)}, bf16[256,768]{1,0:T(8,128)(2,1)}, u32[]{:S(2)}) copy-start(bf16[256,768]{1,0:T(8,128)(2,1)} %get-tuple-element.19) | copy-start | bytes 1179652
  206.3 14.1 %collective-permute-start.1 = (bf16[256,32]{1,0:T(8,128)(2,1)S(1)}, bf16[256,32]{1,0:T(8,128)(2,1)S(1)}, u32[]{:S(2)}, u32[]{:S(2)}) collective-permute-start(bf16[256,32]{1,0:T(8,128)(2,1)S(1)} %get-tuple-element.24), channel_id=1, source_target_pairs={{0,8},{1,9},{2,10},{3,11},{4,12},{5,13},{6,14},{7,15},{8,0},{9,1},... | collective-permute-start | bytes 49160 | tf_op jit(solution)/shard_map/ppermute | solution.py:249
  221.7 14.1 %collective-permute-start.2 = (f32[32,4096]{1,0:T(8,128)S(1)}, f32[32,4096]{1,0:T(8,128)S(1)}, u32[]{:S(2)}, u32[]{:S(2)}) collective-permute-start(f32[32,4096]{1,0:T(8,128)S(1)} %get-tuple-element.27), channel_id=1, source_target_pairs={{0,8},{1,9},{2,10},{3,11},{4,12},{5,13},{6,14},{7,15},{8,0},{9,1},... | collective-permute-start | bytes 1572872 | tf_op jit(solution)/shard_map/ppermute | solution.py:252

commit v5 on v4

--- a/solution.py
+++ b/solution.py
@@ -146,7 +146,7 @@
     )(low, hidden)
 
 
-def finish_kernel(base, wide_low, wide_hidden, wide_out, grad_start, in_start, grad, in_grad, total):
+def finish_kernel(base, wide_low, wide_hidden, own_out, grad_start, grad, in_grad, total):
     step = pl.program_id(0)
     block, width = base.shape
     parts, rank_width = SLOTS // BASE, grad.shape[0]
@@ -159,8 +159,12 @@
             preferred_element_type=jnp.float32,
         )
         total[:, columns] = new + jnp.where(step == 0, 0.0, total[:, columns])
+    wide_out = [own_out[:, at * width : (at + 1) * width] for at in range(parts)]
     halves = lax.dot_general(
-        base[...], wide_out[...], (((1,), (1,)), ((), ())), preferred_element_type=jnp.float32
+        base[...],
+        jnp.concatenate(wide_out, axis=0),
+        (((1,), (1,)), ((), ())),
+        preferred_element_type=jnp.float32,
     )
     back = halves[:, :rank_width]
     for at in range(1, parts):
@@ -172,7 +176,7 @@
         back, wide_hidden[...], (((0,), (0,)), ((), ())), preferred_element_type=jnp.float32
     )
 
-    in_grad[...] = new_in + jnp.where(step == 0, in_start[...], in_grad[...])
+    in_grad[...] = new_in + jnp.where(step == 0, 0.0, in_grad[...])
 
     @pl.when(step == pl.num_programs(0) - 1)
     def _():
@@ -182,23 +186,22 @@
             grad[:, columns] = grad_start[:, columns] + total[rows, :]
 
 
-def finish(base, wide_low, wide_hidden, wide_out, grad_start, in_start):
+def finish(base, wide_low, wide_hidden, own_out, grad_start):
     rows, width = base.shape
     block = rows // 2
+    rank_width, hidden_width = own_out.shape[0], wide_hidden.shape[1]
     row_block = lambda array: pl.BlockSpec((block, array.shape[1]), lambda i: (i, 0))
-    kept = lambda array: pl.BlockSpec(array.shape, lambda i: (0, 0))
+    kept = lambda shape: pl.BlockSpec(shape, lambda i: (0, 0))
+    out_shapes = (grad_start.shape, (rank_width, hidden_width))
     return pl.pallas_call(
         finish_kernel,
         grid=(rows // block,),
         in_specs=[row_block(base), row_block(wide_low), row_block(wide_hidden)]
-        + [kept(wide_out), kept(grad_start), kept(in_start)],
-        out_specs=[kept(grad_start), kept(in_start)],
-        out_shape=[
-            jax.ShapeDtypeStruct(grad_start.shape, jnp.float32),
-            jax.ShapeDtypeStruct(in_start.shape, jnp.float32),
-        ],
-        scratch_shapes=[pltpu.VMEM((wide_out.shape[0], width), jnp.float32)],
-    )(base, wide_low, wide_hidden, wide_out, grad_start, in_start)
+        + [kept(own_out.shape), kept(grad_start.shape)],
+        out_specs=[kept(shape) for shape in out_shapes],
+        out_shape=[jax.ShapeDtypeStruct(shape, jnp.float32) for shape in out_shapes],
+        scratch_shapes=[pltpu.VMEM((wide_low.shape[1], width), jnp.float32)],
+    )(base, wide_low, wide_hidden, own_out, grad_start)
 
 
 def exchange(block):
@@ -214,7 +217,6 @@
     half = n_expert // 2
     pairs = [(i, i ^ half) for i in range(n_expert)]
     own_index = lax.axis_index("dp") * n_expert + lax.axis_index("expert")
-    own_marked = lax.dynamic_index_in_dim(hot_marks, own_index, 0, keepdims=False) == 1
     own_in, own_out = adapter_in[0], adapter_out[0]
 
     partner_out = lax.ppermute(own_out, "expert", pairs)
@@ -224,10 +226,12 @@
         router_probs.T,
         hot_marks[None, :],
         cap_counts[None, :],
-        own_marked.astype(jnp.int32).reshape(1, 1),
+        own_index.reshape(1, 1),
     )
     first, second = pack(half, room, tables, (tokens, cotangent))
     first = exchange(first)
+    own_index += jnp.isnan(first[0, 0, 0]).astype(jnp.int32)
+    own_marked = lax.dynamic_index_in_dim(hot_marks, own_index, 0, keepdims=False) == 1
     second = exchange(second)
 
     inputs = first[:, :, :model_width].reshape(experts * SLOTS, model_width)
@@ -249,23 +253,18 @@
     swapped = lax.ppermute(jnp.where(own_marked, far_low, extra_back), "expert", pairs)
     extra_low = jnp.where(own_marked, own_low, swapped)
     extra_grad = jnp.einsum("nr,nd->rd", extra_low, extra, preferred_element_type=jnp.float32)
-    returned = lax.ppermute(extra_grad, "expert", pairs)
+    returned = lax.ppermute(extra_grad.astype(jnp.bfloat16), "expert", pairs)
     in_start = jnp.einsum("nr,nf->rf", extra_back, own_hidden, preferred_element_type=jnp.float32)
     in_start += jnp.einsum("nr,nf->rf", swapped, far_hidden, preferred_element_type=jnp.float32)
-
-    parts, width = SLOTS // BASE, BASE * model_width // SLOTS
-    wide_out = jnp.concatenate(
-        [own_out[:, at * width : (at + 1) * width] for at in range(parts)], axis=0
-    )
     grad, in_grad = finish(
-        second.reshape(experts * SLOTS, width),
+        second.reshape(experts * SLOTS, BASE * model_width // SLOTS),
         wide_low,
         wide_hidden,
-        wide_out,
+        own_out,
         jnp.where(own_marked, extra_grad, 0.0),
-        jnp.where(own_marked, in_start, 0.0),
-    )
-    out_grad = grad + jnp.where(own_marked, returned, 0.0)
+    )
+    in_grad = in_grad + jnp.where(own_marked, in_start, 0.0)
+    out_grad = grad + jnp.where(own_marked, returned.astype(jnp.float32), 0.0)
     return in_grad[None], out_grad[None]
 
 

time: 240 us -> 233 us (0.971)
  waiting for transfers between devices: 154 us -> 145 us
    ppermute x1, waiting for transfers between devices: 5.92 us -> 0.01 us  [layer(): returned = lax.ppermute(extra_grad.astype(jnp.bfloat16), 'expert', pairs)]
    ppermute x1, waiting for transfers between devices: 11.3 us -> 7.75 us  [layer(): lax.ppermute(jnp.where(own_marked, far_low, extra_back), 'expert', pairs)]
  transfers between devices with their start and end apart: 5 -> 5, of which waited for: 3 -> 2; matrix products, arithmetic and copies ran while one was open for 14% -> 15% of each run, Pallas kernels for 4% -> 5%
where the time goes in v5:
time: 233 us; the launch traced here: 231 us
  waiting for transfers between devices  145 us (62%)
  starting transfers between devices  26.2 us (11%)
  matrix products  25.7 us (11%)
  Pallas kernels  19.9 us (9%)
  local copies, waits for them, and re-layouts  8.16 us (4%)
  other arithmetic  3.43 us (1%)
  between operations  2.69 us (1%)
    all_to_all x2, waiting for transfers between devices, exchange(): return lax.all_to_all(block, AXES, split_axis=0, concat_axis=0, tiled=True)  137 us
    all_to_all x2, starting transfers between devices, exchange(): return lax.all_to_all(block, AXES, split_axis=0, concat_axis=0, tiled=True)  19.6 us
    dot_general x1, matrix products, layer(): up_out = jnp.dot(inputs, gate_up[0, 1], preferred_element_type=jnp.float32)  11.1 us
    dot_general x1, matrix products, layer(): jnp.dot(inputs, gate_up[0, 0], preferred_element_type=jnp.float32)  10.9 us
    pallas_call x1, Pallas kernels, pack(): pl.pallas_call(functools.partial(pack_kernel, half, room), grid=(experts...  9.44 us
    ppermute x1, waiting for transfers between devices, layer(): lax.ppermute(jnp.where(own_marked, far_low, extra_back), 'expert', pairs)  7.75 us
    pallas_call x1, Pallas kernels, finish(): pl.pallas_call(finish_kernel, grid=(rows // block,), in_specs=[row_block(...  6.01 us
  transfers between devices with their start and end apart: 5, of which 2 were waited for; matrix products, arithmetic and copies ran while one was open for 15% of the time, Pallas kernels for 5%

profile of v5, /device:TPU:5, one launch (start us, length us, event | category | flops | bytes accessed | tf_op | source)
XLA Modules:
  0.0 230.9 jit_solution(11547995482536699560)
XLA Ops:
  0.6 0.0 copy-start
  0.7 9.4 %shard_map.104 = (bf16[128,8,5120]{2,1,0:T(8,128)(2,1)}, bf16[128,8,2048]{2,1,0:T(8,128)(2,1)}) custom-call(s32[4,128]{1,0:T(4,128)} %bitcast.45, f32[4,128]{1,0:T(4,128)} %bitcast.46, s32[1,128]{1,0:T(1,128)} %bitcast.48, s32[1,128]{1,0:T(1,128)} %bitcast.47, s32[1,1]{1,0:T(1,128)} %bitcast.4.own, bf16[128,4096]{1,0:T(8,128)(2,1)} %tokens.1, ...), custom_call_target="tpu_custom_call" | custom-call | tf_op jit(solution)/shard_map/pallas_call | solution.py:94
  10.1 11.2 %all-to-all-start.1 = ((bf16[128,8,5120]{2,1,0:T(8,128)(2,1)}), bf16[128,8,5120]{2,1,0:T(8,128)(2,1)}, u32[]{:S(2)}, u32[]{:S(2)}) async-start(bf16[128,8,5120]{2,1,0:T(8,128)(2,1)} %get-tuple-element.13), calls=%async_computation.1 | async-start | bytes 20971520 | tf_op jit(solution)/shard_map/all_to_all | solution.py:208
  21.3 0.0 copy-done.4
  21.3 2.8 %collective-permute-start = (bf16[32,4096]{1,0:T(8,128)(2,1)S(1)}, bf16[32,4096]{1,0:T(8,128)(2,1)S(1)}, u32[]{:S(2)}, u32[]{:S(2)}) collective-permute-start(bf16[32,4096]{1,0:T(8,128)(2,1)S(1)} %bitcast.44), channel_id=1, source_target_pairs={{0,8},{1,9},{2,10},{3,11},{4,12},{5,13},{6,14},{7,15},{8,0},{9,1},... | collective-permute-start | bytes 786440 | tf_op jit(solution)/shard_map/ppermute | solution.py:222
  24.1 137.2 %all-to-all-done.1 = bf16[128,8,5120]{2,1,0:T(8,128)(2,1)} async-done(((bf16[128,8,5120]{2,1,0:T(8,128)(2,1)}), bf16[128,8,5120]{2,1,0:T(8,128)(2,1)}, u32[]{:S(2)}, u32[]{:S(2)}) %all-to-all-start.1) | async-done | bytes 10485792 | tf_op jit(solution)/shard_map/all_to_all | solution.py:208
  161.3 8.5 %all-to-all-start = ((bf16[128,8,2048]{2,1,0:T(8,128)(2,1)}), bf16[128,8,2048]{2,1,0:T(8,128)(2,1)}, u32[]{:S(2)}, u32[]{:S(2)}) async-start(bf16[128,8,2048]{2,1,0:T(8,128)(2,1)} %get-tuple-element.12), calls=%async_computation | async-start | bytes 8388608 | tf_op jit(solution)/shard_map/all_to_all | solution.py:208
  169.8 10.9 %fusion.1 = f32[1024,768]{1,0:T(8,128)S(1)} fusion(bf16[128,8,5120]{2,1,0:T(8,128)(2,1)} %all-to-all-done.1, bf16[1,2,4096,768]{3,2,1,0:T(8,128)(2,1)} %param.15), kind=kOutput, calls=%fused_computation.2 | convolution fusion | flops 6442450944 | bytes 17825792 | tf_op jit(solution)/shard_map/dot_general | solution.py:238
  180.7 11.1 %multiply_convert_fusion.hidden = bf16[1024,768]{1,0:T(8,128)(2,1)S(1)} fusion(f32[1024,768]{1,0:T(8,128)S(1)} %fusion.1, bf16[1,2,4096,768]{3,2,1,0:T(8,128)(2,1)} %param.15, bf16[128,8,5120]{2,1,0:T(8,128)(2,1)} %all-to-all-done.1), kind=kOutput, calls=%fused_computation.7 | convolution fusion | flops 6447169536 | bytes 19398656 | tf_op jit(solution)/shard_map/dot_general | solution.py:239
  191.8 0.0 copy-done
  191.8 0.0 copy-start.6
  191.8 1.3 fusion.8.low
  193.1 4.4 %shard_map.105 = (bf16[1024,64]{1,0:T(8,128)(2,1)}, bf16[1024,768]{1,0:T(8,128)(2,1)}, bf16[256,32]{1,0:T(8,128)(2,1)}, bf16[256,768]{1,0:T(8,128)(2,1)}, bf16[2...) custom-call(bf16[1024,32]{1,0:T(8,128)(2,1)} %fusion.8.low, bf16[1024,768]{1,0:T(8,128)(2,1)} %copy-done.1), custom_call_target="tpu_custom_call" | custom-call | tf_op jit(solution)/shard_map/pallas_call | solution.py:140
  197.5 1.3 slice.21
  200.1 0.0 copy-done.6
  200.1 0.7 dynamic_slice.4
  200.7 3.1 %slice.22 = bf16[128,8,1024]{2,1,0:T(8,128)(2,1)} slice(bf16[128,8,5120]{2,1,0:T(8,128)(2,1)} %all-to-all-done.1), slice={[0:128], [0:8], [4096:5120]} | slice | bytes 4194304 | tf_op jit(solution)/shard_map/slice | solution.py:247
  203.8 3.2 %reshape_reshape.3 = bf16[256,4096]{1,0:T(8,128)(2,1)S(1)} reshape(bf16[128,8,1024]{2,1,0:T(8,128)(2,1)} %slice.22) | data formatting | bytes 4194304 | tf_op jit(solution)/shard_map/reshape;reshape | solution.py:248
  207.6 0.0 collective-permute-done
  207.6 0.7 broadcast_select_fusion.1
  208.3 2.8 %collective-permute-start.1 = (bf16[256,32]{1,0:T(8,128)(2,1)S(1)}, bf16[256,32]{1,0:T(8,128)(2,1)S(1)}, u32[]{:S(2)}, u32[]{:S(2)}) collective-permute-start(bf16[256,32]{1,0:T(8,128)(2,1)S(1)} %get-tuple-element.24), channel_id=1, source_target_pairs={{0,8},{1,9},{2,10},{3,11},{4,12},{5,13},{6,14},{7,15},{8,0},{9,1},... | collective-permute-start | bytes 49160 | tf_op jit(solution)/shard_map/ppermute | solution.py:253
  211.1 0.0 copy-done.3
  211.1 0.2 fusion.19
  211.3 7.7 %collective-permute-done.1 = bf16[256,32]{1,0:T(8,128)(2,1)S(1)} collective-permute-done((bf16[256,32]{1,0:T(8,128)(2,1)S(1)}, bf16[256,32]{1,0:T(8,128)(2,1)S(1)}, u32[]{:S(2)}, u32[]{:S(2)}) %collective-permute-start.1) | collective-permute-done | bytes 16416 | tf_op jit(solution)/shard_map/ppermute | solution.py:253
  219.1 1.3 fusion.18
  220.3 0.9 collective-permute-start.2
  221.3 0.2 fusion.10
  221.5 0.0 all-to-all-done
  221.5 6.0 %shard_map.106 = (f32[32,4096]{1,0:T(8,128)}, f32[32,768]{1,0:T(8,128)}) custom-call(bf16[1024,2048]{1,0:T(8,128)(2,1)} %bitcast.5.base, bf16[1024,64]{1,0:T(8,128)(2,1)} %get-tuple-element.14.wide_low, bf16[1024,768]{1,0:T(8,128)(2,1)} %get-tuple-element.15.wide_hidden, bf16[32,4096]{1,0:T(8,128)(2,1)} %bitcast.43, f32[32,4096]{1,0:T(8,128)} %get-tuple-element.23.grad_start), custom_call_target="tpu_custom_call" | custom-call | tf_op jit(solution)/shard_map/pallas_call | solution.py:196
  227.5 1.5 add_bitcast_fusion.1
  229.1 0.0 collective-permute-done.2
  229.1 1.9 add_bitcast_fusion
  (10 shorter events, 0.0 us)
Async XLA Ops:
  0.6 191.2 %copy-start = (bf16[1,32,768]{2,1,0:T(8,128)(2,1)S(1)}, bf16[1,32,768]{2,1,0:T(8,128)(2,1)}, u32[]{:S(2)}) copy-start(bf16[1,32,768]{2,1,0:T(8,128)(2,1)} %param.16) | copy-start | bytes 147460
  10.1 11.2 %copy-start.4 = (bf16[1,32,4096]{2,1,0:T(8,128)(2,1)S(1)}, bf16[1,32,4096]{2,1,0:T(8,128)(2,1)}, u32[]{:S(2)}) copy-start(bf16[1,32,4096]{2,1,0:T(8,128)(2,1)} %param.17) | copy-start | bytes 786436
  10.1 151.2 %all-to-all-start.1 = ((bf16[128,8,5120]{2,1,0:T(8,128)(2,1)}), bf16[128,8,5120]{2,1,0:T(8,128)(2,1)}, u32[]{:S(2)}, u32[]{:S(2)}) async-start(bf16[128,8,5120]{2,1,0:T(8,128)(2,1)} %get-tuple-element.13), calls=%async_computation.1 | async-start | bytes 20971520 | tf_op jit(solution)/shard_map/all_to_all | solution.py:208
  21.3 186.3 %collective-permute-start = (bf16[32,4096]{1,0:T(8,128)(2,1)S(1)}, bf16[32,4096]{1,0:T(8,128)(2,1)S(1)}, u32[]{:S(2)}, u32[]{:S(2)}) collective-permute-start(bf16[32,4096]{1,0:T(8,128)(2,1)S(1)} %bitcast.44), channel_id=1, source_target_pairs={{0,8},{1,9},{2,10},{3,11},{4,12},{5,13},{6,14},{7,15},{8,0},{9,1},... | collective-permute-start | bytes 786440 | tf_op jit(solution)/shard_map/ppermute | solution.py:222
  161.3 60.2 %all-to-all-start = ((bf16[128,8,2048]{2,1,0:T(8,128)(2,1)}), bf16[128,8,2048]{2,1,0:T(8,128)(2,1)}, u32[]{:S(2)}, u32[]{:S(2)}) async-start(bf16[128,8,2048]{2,1,0:T(8,128)(2,1)} %get-tuple-element.12), calls=%async_computation | async-start | bytes 8388608 | tf_op jit(solution)/shard_map/all_to_all | solution.py:208
  191.8 1.3 copy-start.1
  191.8 8.2 %copy-start.6 = (s32[128]{0:T(128)S(1)}, s32[128]{0:T(128)}, u32[]{:S(2)}) copy-start(s32[128]{0:T(128)} %param.13) | copy-start | bytes 1540
  203.8 3.8 %copy-start.7 = (bf16[256,32]{1,0:T(8,128)(2,1)S(1)}, bf16[256,32]{1,0:T(8,128)(2,1)}, u32[]{:S(2)}) copy-start(bf16[256,32]{1,0:T(8,128)(2,1)} %get-tuple-element.17) | copy-start | bytes 49156
  203.8 7.3 %copy-start.3 = (bf16[256,768]{1,0:T(8,128)(2,1)S(1)}, bf16[256,768]{1,0:T(8,128)(2,1)}, u32[]{:S(2)}) copy-start(bf16[256,768]{1,0:T(8,128)(2,1)} %get-tuple-element.19) | copy-start | bytes 1179652
  203.8 15.3 %copy-start.5 = (bf16[256,32]{1,0:T(8,128)(2,1)S(1)}, bf16[256,32]{1,0:T(8,128)(2,1)}, u32[]{:S(2)}) copy-start(bf16[256,32]{1,0:T(8,128)(2,1)} %get-tuple-element.16) | copy-start | bytes 49156
  207.6 13.7 %copy-start.2 = (bf16[256,768]{1,0:T(8,128)(2,1)S(1)}, bf16[256,768]{1,0:T(8,128)(2,1)}, u32[]{:S(2)}) copy-start(bf16[256,768]{1,0:T(8,128)(2,1)} %get-tuple-element.20) | copy-start | bytes 1179652
  208.3 10.7 %collective-permute-start.1 = (bf16[256,32]{1,0:T(8,128)(2,1)S(1)}, bf16[256,32]{1,0:T(8,128)(2,1)S(1)}, u32[]{:S(2)}, u32[]{:S(2)}) collective-permute-start(bf16[256,32]{1,0:T(8,128)(2,1)S(1)} %get-tuple-element.24), channel_id=1, source_target_pairs={{0,8},{1,9},{2,10},{3,11},{4,12},{5,13},{6,14},{7,15},{8,0},{9,1},... | collective-permute-start | bytes 49160 | tf_op jit(solution)/shard_map/ppermute | solution.py:253
  220.3 8.7 %collective-permute-start.2 = (bf16[32,4096]{1,0:T(8,128)(2,1)S(1)}, bf16[32,4096]{1,0:T(8,128)(2,1)S(1)}, u32[]{:S(2)}, u32[]{:S(2)}) collective-permute-start(bf16[32,4096]{1,0:T(8,128)(2,1)S(1)} %get-tuple-element.22), channel_id=1, source_target_pairs={{0,8},{1,9},{2,10},{3,11},{4,12},{5,13},{6,14},{7,15},{8,0},{9,1},... | collective-permute-start | bytes 786440 | tf_op jit(solution)/shard_map/ppermute | solution.py:256

commit v6 on v5

--- a/solution.py
+++ b/solution.py
@@ -146,7 +146,19 @@
     )(low, hidden)
 
 
-def finish_kernel(base, wide_low, wide_hidden, own_out, grad_start, grad, in_grad, total):
+def finish_kernel(
+    base,
+    wide_low,
+    wide_hidden,
+    own_out,
+    near_back,
+    near_hidden,
+    far_back,
+    far_hidden,
+    grad,
+    in_grad,
+    total,
+):
     step = pl.program_id(0)
     block, width = base.shape
     parts, rank_width = SLOTS // BASE, grad.shape[0]
@@ -176,32 +188,47 @@
         back, wide_hidden[...], (((0,), (0,)), ((), ())), preferred_element_type=jnp.float32
     )
 
-    in_grad[...] = new_in + jnp.where(step == 0, 0.0, in_grad[...])
+
+    @pl.when(step == 0)
+    def _():
+        start = new_in
+        for back_rows, hidden_rows in ((near_back, near_hidden), (far_back, far_hidden)):
+            start = start + lax.dot_general(
+                back_rows[...],
+                hidden_rows[...],
+                (((0,), (0,)), ((), ())),
+                preferred_element_type=jnp.float32,
+            )
+        in_grad[...] = start
+
+    @pl.when(step > 0)
+    def _():
+        in_grad[...] += new_in
 
     @pl.when(step == pl.num_programs(0) - 1)
     def _():
         for at in range(parts):
             columns = slice(at * width, (at + 1) * width)
             rows = slice(at * rank_width, (at + 1) * rank_width)
-            grad[:, columns] = grad_start[:, columns] + total[rows, :]
-
-
-def finish(base, wide_low, wide_hidden, own_out, grad_start):
+            grad[:, columns] = total[rows, :]
+
+
+def finish(base, wide_low, wide_hidden, *whole):
     rows, width = base.shape
     block = rows // 2
-    rank_width, hidden_width = own_out.shape[0], wide_hidden.shape[1]
+    own_out = whole[0]
     row_block = lambda array: pl.BlockSpec((block, array.shape[1]), lambda i: (i, 0))
     kept = lambda shape: pl.BlockSpec(shape, lambda i: (0, 0))
-    out_shapes = (grad_start.shape, (rank_width, hidden_width))
+    out_shapes = (own_out.shape, (own_out.shape[0], wide_hidden.shape[1]))
     return pl.pallas_call(
         finish_kernel,
         grid=(rows // block,),
-        in_specs=[row_block(base), row_block(wide_low), row_block(wide_hidden)]
-        + [kept(own_out.shape), kept(grad_start.shape)],
+        in_specs=[row_block(x) for x in (base, wide_low, wide_hidden)]
+        + [kept(x.shape) for x in whole],
         out_specs=[kept(shape) for shape in out_shapes],
         out_shape=[jax.ShapeDtypeStruct(shape, jnp.float32) for shape in out_shapes],
         scratch_shapes=[pltpu.VMEM((wide_low.shape[1], width), jnp.float32)],
-    )(base, wide_low, wide_hidden, own_out, grad_start)
+    )(base, wide_low, wide_hidden, *whole)
 
 
 def exchange(block):
@@ -254,17 +281,17 @@
     extra_low = jnp.where(own_marked, own_low, swapped)
     extra_grad = jnp.einsum("nr,nd->rd", extra_low, extra, preferred_element_type=jnp.float32)
     returned = lax.ppermute(extra_grad.astype(jnp.bfloat16), "expert", pairs)
-    in_start = jnp.einsum("nr,nf->rf", extra_back, own_hidden, preferred_element_type=jnp.float32)
-    in_start += jnp.einsum("nr,nf->rf", swapped, far_hidden, preferred_element_type=jnp.float32)
     grad, in_grad = finish(
         second.reshape(experts * SLOTS, BASE * model_width // SLOTS),
         wide_low,
         wide_hidden,
         own_out,
-        jnp.where(own_marked, extra_grad, 0.0),
-    )
-    in_grad = in_grad + jnp.where(own_marked, in_start, 0.0)
-    out_grad = grad + jnp.where(own_marked, returned.astype(jnp.float32), 0.0)
+        extra_back,
+        own_hidden,
+        swapped,
+        far_hidden,
+    )
+    out_grad = grad + jnp.where(own_marked, extra_grad + returned.astype(jnp.float32), 0.0)
     return in_grad[None], out_grad[None]
 
 

time: 233 us -> 232 us (level)
  transfers between devices with their start and end apart: 5 -> 5, of which waited for: 2 -> 4; matrix products, arithmetic and copies ran while one was open for 15% -> 14% of each run, Pallas kernels for 5% -> 5%
where the time goes in v6:
time: 232 us; the launch traced here: 231 us
  waiting for transfers between devices  147 us (63%)
  starting transfers between devices  25.8 us (11%)
  matrix products  25 us (11%)
  Pallas kernels  20.2 us (9%)
  local copies, waits for them, and re-layouts  8 us (3%)
  between operations  2.71 us (1%)
    all_to_all x2, waiting for transfers between devices, exchange(): return lax.all_to_all(block, AXES, split_axis=0, concat_axis=0, tiled=True)  138 us
    all_to_all x2, starting transfers between devices, exchange(): return lax.all_to_all(block, AXES, split_axis=0, concat_axis=0, tiled=True)  19.6 us
    dot_general x1, matrix products, layer(): up_out = jnp.dot(inputs, gate_up[0, 1], preferred_element_type=jnp.float32)  11.1 us
    dot_general x1, matrix products, layer(): jnp.dot(inputs, gate_up[0, 0], preferred_element_type=jnp.float32)  10.9 us
    pallas_call x1, Pallas kernels, pack(): pl.pallas_call(functools.partial(pack_kernel, half, room), grid=(experts...  9.47 us
    ppermute x1, waiting for transfers between devices, layer(): lax.ppermute(jnp.where(own_marked, far_low, extra_back), 'expert', pairs)  7.95 us
    pallas_call x1, Pallas kernels, finish(): pl.pallas_call(finish_kernel, grid=(rows // block,), in_specs=[row_block(...  6.29 us
  transfers between devices with their start and end apart: 5, of which 4 were waited for; matrix products, arithmetic and copies ran while one was open for 14% of the time, Pallas kernels for 5%

profile of v6, /device:TPU:5, one launch (start us, length us, event | category | flops | bytes accessed | tf_op | source)
XLA Modules:
  0.0 230.8 jit_solution(1177537580612243577)
XLA Ops:
  0.6 0.0 copy-start
  0.7 9.5 %shard_map.104 = (bf16[128,8,5120]{2,1,0:T(8,128)(2,1)}, bf16[128,8,2048]{2,1,0:T(8,128)(2,1)}) custom-call(s32[4,128]{1,0:T(4,128)} %bitcast.40, f32[4,128]{1,0:T(4,128)} %bitcast.41, s32[1,128]{1,0:T(1,128)} %bitcast.43, s32[1,128]{1,0:T(1,128)} %bitcast.42, s32[1,1]{1,0:T(1,128)} %bitcast.4.own, bf16[128,4096]{1,0:T(8,128)(2,1)} %tokens.1, ...), custom_call_target="tpu_custom_call" | custom-call | tf_op jit(solution)/shard_map/pallas_call | solution.py:94
  10.1 11.2 %all-to-all-start.1 = ((bf16[128,8,5120]{2,1,0:T(8,128)(2,1)}), bf16[128,8,5120]{2,1,0:T(8,128)(2,1)}, u32[]{:S(2)}, u32[]{:S(2)}) async-start(bf16[128,8,5120]{2,1,0:T(8,128)(2,1)} %get-tuple-element.13), calls=%async_computation.1 | async-start | bytes 20971520 | tf_op jit(solution)/shard_map/all_to_all | solution.py:235
  21.3 0.0 copy-done.2
  21.3 2.8 %collective-permute-start = (bf16[32,4096]{1,0:T(8,128)(2,1)S(1)}, bf16[32,4096]{1,0:T(8,128)(2,1)S(1)}, u32[]{:S(2)}, u32[]{:S(2)}) collective-permute-start(bf16[32,4096]{1,0:T(8,128)(2,1)S(1)} %bitcast.39), channel_id=1, source_target_pairs={{0,8},{1,9},{2,10},{3,11},{4,12},{5,13},{6,14},{7,15},{8,0},{9,1},... | collective-permute-start | bytes 786440 | tf_op jit(solution)/shard_map/ppermute | solution.py:249
  24.1 137.2 %all-to-all-done.1 = bf16[128,8,5120]{2,1,0:T(8,128)(2,1)} async-done(((bf16[128,8,5120]{2,1,0:T(8,128)(2,1)}), bf16[128,8,5120]{2,1,0:T(8,128)(2,1)}, u32[]{:S(2)}, u32[]{:S(2)}) %all-to-all-start.1) | async-done | bytes 10485792 | tf_op jit(solution)/shard_map/all_to_all | solution.py:235
  161.3 8.5 %all-to-all-start = ((bf16[128,8,2048]{2,1,0:T(8,128)(2,1)}), bf16[128,8,2048]{2,1,0:T(8,128)(2,1)}, u32[]{:S(2)}, u32[]{:S(2)}) async-start(bf16[128,8,2048]{2,1,0:T(8,128)(2,1)} %get-tuple-element.12), calls=%async_computation | async-start | bytes 8388608 | tf_op jit(solution)/shard_map/all_to_all | solution.py:235
  169.8 10.9 %fusion.1 = f32[1024,768]{1,0:T(8,128)S(1)} fusion(bf16[128,8,5120]{2,1,0:T(8,128)(2,1)} %all-to-all-done.1, bf16[1,2,4096,768]{3,2,1,0:T(8,128)(2,1)} %param.15), kind=kOutput, calls=%fused_computation.2 | convolution fusion | flops 6442450944 | bytes 17825792 | tf_op jit(solution)/shard_map/dot_general | solution.py:265
  180.7 11.1 %multiply_convert_fusion.hidden = bf16[1024,768]{1,0:T(8,128)(2,1)S(1)} fusion(f32[1024,768]{1,0:T(8,128)S(1)} %fusion.1, bf16[1,2,4096,768]{3,2,1,0:T(8,128)(2,1)} %param.15, bf16[128,8,5120]{2,1,0:T(8,128)(2,1)} %all-to-all-done.1), kind=kOutput, calls=%fused_computation.7 | convolution fusion | flops 6447169536 | bytes 19398656 | tf_op jit(solution)/shard_map/dot_general | solution.py:266
  191.8 0.0 copy-done
  191.8 0.0 copy-start.1
  191.8 0.0 copy-start.5
  191.8 1.2 fusion.8.low
  193.1 0.0 copy-done.1
  193.1 4.4 %shard_map.105 = (bf16[1024,64]{1,0:T(8,128)(2,1)}, bf16[1024,768]{1,0:T(8,128)(2,1)}, bf16[256,32]{1,0:T(8,128)(2,1)}, bf16[256,768]{1,0:T(8,128)(2,1)}, bf16[2...) custom-call(bf16[1024,32]{1,0:T(8,128)(2,1)} %fusion.8.low, bf16[1024,768]{1,0:T(8,128)(2,1)} %copy-done.1), custom_call_target="tpu_custom_call" | custom-call | tf_op jit(solution)/shard_map/pallas_call | solution.py:140
  197.5 1.2 slice.22
  200.0 0.0 copy-done.5
  200.0 0.6 dynamic_slice.4
  200.6 3.1 %slice.21 = bf16[128,8,1024]{2,1,0:T(8,128)(2,1)} slice(bf16[128,8,5120]{2,1,0:T(8,128)(2,1)} %all-to-all-done.1), slice={[0:128], [0:8], [4096:5120]} | slice | bytes 4194304 | tf_op jit(solution)/shard_map/slice | solution.py:274
  203.7 3.1 %reshape_reshape.3 = bf16[256,4096]{1,0:T(8,128)(2,1)S(1)} reshape(bf16[128,8,1024]{2,1,0:T(8,128)(2,1)} %slice.21) | data formatting | bytes 4194304 | tf_op jit(solution)/shard_map/reshape;reshape | solution.py:275
  207.4 0.0 collective-permute-done
  207.5 0.0 copy-done.6
  207.5 1.3 broadcast_select_fusion
  208.8 2.7 %collective-permute-start.1 = (bf16[256,32]{1,0:T(8,128)(2,1)S(1)}, bf16[256,32]{1,0:T(8,128)(2,1)S(1)}, u32[]{:S(2)}, u32[]{:S(2)}) collective-permute-start(bf16[256,32]{1,0:T(8,128)(2,1)S(1)} %get-tuple-element.22), channel_id=1, source_target_pairs={{0,8},{1,9},{2,10},{3,11},{4,12},{5,13},{6,14},{7,15},{8,0},{9,1},... | collective-permute-start | bytes 49160 | tf_op jit(solution)/shard_map/ppermute | solution.py:280
  211.5 8.0 %collective-permute-done.1.far_back = bf16[256,32]{1,0:T(8,128)(2,1)S(1)} collective-permute-done((bf16[256,32]{1,0:T(8,128)(2,1)S(1)}, bf16[256,32]{1,0:T(8,128)(2,1)S(1)}, u32[]{:S(2)}, u32[]{:S(2)}) %collective-permute-start.1) | collective-permute-done | bytes 16416 | tf_op jit(solution)/shard_map/ppermute | solution.py:280
  219.4 0.0 copy-done.4
  219.4 0.5 fusion.17
  219.9 0.6 collective-permute-start.2
  220.6 0.5 all-to-all-done
  221.1 6.3 %shard_map.106 = (f32[32,4096]{1,0:T(8,128)}, f32[32,768]{1,0:T(8,128)}) custom-call(bf16[1024,2048]{1,0:T(8,128)(2,1)} %bitcast.5.base, bf16[1024,64]{1,0:T(8,128)(2,1)} %get-tuple-element.14.wide_low, bf16[1024,768]{1,0:T(8,128)(2,1)} %get-tuple-element.15.wide_hidden, bf16[32,4096]{1,0:T(8,128)(2,1)} %bitcast.38, ...), custom_call_target="tpu_custom_call" | custom-call | tf_op jit(solution)/shard_map/pallas_call | solution.py:223
  227.4 1.5 collective-permute-done.2
  228.9 1.9 add_bitcast_fusion
  (5 shorter events, 0.0 us)
Async XLA Ops:
  0.6 191.2 %copy-start = (bf16[1,32,768]{2,1,0:T(8,128)(2,1)S(1)}, bf16[1,32,768]{2,1,0:T(8,128)(2,1)}, u32[]{:S(2)}) copy-start(bf16[1,32,768]{2,1,0:T(8,128)(2,1)} %param.16) | copy-start | bytes 147460
  10.1 11.2 %copy-start.2 = (bf16[1,32,4096]{2,1,0:T(8,128)(2,1)S(1)}, bf16[1,32,4096]{2,1,0:T(8,128)(2,1)}, u32[]{:S(2)}) copy-start(bf16[1,32,4096]{2,1,0:T(8,128)(2,1)} %param.17) | copy-start | bytes 786436
  10.1 151.2 %all-to-all-start.1 = ((bf16[128,8,5120]{2,1,0:T(8,128)(2,1)}), bf16[128,8,5120]{2,1,0:T(8,128)(2,1)}, u32[]{:S(2)}, u32[]{:S(2)}) async-start(bf16[128,8,5120]{2,1,0:T(8,128)(2,1)} %get-tuple-element.13), calls=%async_computation.1 | async-start | bytes 20971520 | tf_op jit(solution)/shard_map/all_to_all | solution.py:235
  21.3 186.1 %collective-permute-start = (bf16[32,4096]{1,0:T(8,128)(2,1)S(1)}, bf16[32,4096]{1,0:T(8,128)(2,1)S(1)}, u32[]{:S(2)}, u32[]{:S(2)}) collective-permute-start(bf16[32,4096]{1,0:T(8,128)(2,1)S(1)} %bitcast.39), channel_id=1, source_target_pairs={{0,8},{1,9},{2,10},{3,11},{4,12},{5,13},{6,14},{7,15},{8,0},{9,1},... | collective-permute-start | bytes 786440 | tf_op jit(solution)/shard_map/ppermute | solution.py:249
  161.3 59.8 %all-to-all-start = ((bf16[128,8,2048]{2,1,0:T(8,128)(2,1)}), bf16[128,8,2048]{2,1,0:T(8,128)(2,1)}, u32[]{:S(2)}, u32[]{:S(2)}) async-start(bf16[128,8,2048]{2,1,0:T(8,128)(2,1)} %get-tuple-element.12), calls=%async_computation | async-start | bytes 8388608 | tf_op jit(solution)/shard_map/all_to_all | solution.py:235
  191.8 1.3 copy-start.1
  191.8 8.2 %copy-start.5 = (s32[128]{0:T(128)S(1)}, s32[128]{0:T(128)}, u32[]{:S(2)}) copy-start(s32[128]{0:T(128)} %param.13) | copy-start | bytes 1540
  203.6 3.8 %copy-start.6 = (bf16[256,32]{1,0:T(8,128)(2,1)S(1)}, bf16[256,32]{1,0:T(8,128)(2,1)}, u32[]{:S(2)}) copy-start(bf16[256,32]{1,0:T(8,128)(2,1)} %get-tuple-element.17) | copy-start | bytes 49156
  203.7 15.8 %copy-start.4 = (bf16[256,32]{1,0:T(8,128)(2,1)S(1)}, bf16[256,32]{1,0:T(8,128)(2,1)}, u32[]{:S(2)}) copy-start(bf16[256,32]{1,0:T(8,128)(2,1)} %get-tuple-element.21) | copy-start | bytes 49156
  208.8 10.7 %collective-permute-start.1 = (bf16[256,32]{1,0:T(8,128)(2,1)S(1)}, bf16[256,32]{1,0:T(8,128)(2,1)S(1)}, u32[]{:S(2)}, u32[]{:S(2)}) collective-permute-start(bf16[256,32]{1,0:T(8,128)(2,1)S(1)} %get-tuple-element.22), channel_id=1, source_target_pairs={{0,8},{1,9},{2,10},{3,11},{4,12},{5,13},{6,14},{7,15},{8,0},{9,1},... | collective-permute-start | bytes 49160 | tf_op jit(solution)/shard_map/ppermute | solution.py:280
  219.4 1.7 copy-start.3
  219.9 8.9 %collective-permute-start.2 = (bf16[32,4096]{1,0:T(8,128)(2,1)S(1)}, bf16[32,4096]{1,0:T(8,128)(2,1)S(1)}, u32[]{:S(2)}, u32[]{:S(2)}) collective-permute-start(bf16[32,4096]{1,0:T(8,128)(2,1)S(1)} %get-tuple-element.24), channel_id=1, source_target_pairs={{0,8},{1,9},{2,10},{3,11},{4,12},{5,13},{6,14},{7,15},{8,0},{9,1},... | collective-permute-start | bytes 786440 | tf_op jit(solution)/shard_map/ppermute | solution.py:283

commit v7 on v6

--- a/solution.py
+++ b/solution.py
@@ -12,7 +12,7 @@
 SLOTS = 8
 BASE = 4
 EXTRA = 2
-GROUP = 32
+GROUP = 64
 CHUNK = 512
 AXES = ("dp", "expert")
 
@@ -76,14 +76,15 @@
     rows = jnp.dot(
         pick.reshape(GROUP * SLOTS, tok_count), tokens[...], preferred_element_type=jnp.float32
     )
-    first[:, :, :width] = rows.reshape(GROUP, SLOTS, width).astype(jnp.bfloat16)
+    here = pl.ds(pl.program_id(0) * GROUP, GROUP)
+    first[here, :, :width] = rows.reshape(GROUP, SLOTS, width).astype(jnp.bfloat16)
     hot = jnp.where(marked == 1, experts, experts ^ half)
     hot_rank, hot_weight = slot_table(
         hot, routing[...], probs[...], look_up(caps[...], hot) + room
     )
     hot_rank = hot_rank - jnp.where(marked == 1, BASE, BASE + EXTRA)
-    first[:, :, width:] = spread(hot_rank, hot_weight, cotangent, EXTRA)
-    second[...] = spread(rank, weight, cotangent, BASE)
+    first[here, :, width:] = spread(hot_rank, hot_weight, cotangent, EXTRA)
+    second[here, :, :] = spread(rank, weight, cotangent, BASE)
 
 
 def pack(half, room, tables, arrays):
@@ -95,8 +96,9 @@
         functools.partial(pack_kernel, half, room),
         grid=(experts // GROUP,),
         in_specs=[pl.BlockSpec(x.shape, lambda i: (0, 0)) for x in operands],
-        out_specs=[pl.BlockSpec((GROUP, SLOTS, w), lambda i: (i, 0, 0)) for w in widths],
-        out_shape=[jax.ShapeDtypeStruct((experts, SLOTS, w), jnp.bfloat16) for w in widths],
+        out_specs=[pl.BlockSpec(memory_space=pltpu.VMEM) for w in widths],
+        out_shape=[pltpu.VMEM((experts, SLOTS, w), jnp.bfloat16) for w in widths],
+        compiler_params=pltpu.CompilerParams(vmem_limit_bytes=50200 << 10),
     )(*operands)
 
 
@@ -215,7 +217,7 @@
 
 def finish(base, wide_low, wide_hidden, *whole):
     rows, width = base.shape
-    block = rows // 2
+    block = rows // 4
     own_out = whole[0]
     row_block = lambda array: pl.BlockSpec((block, array.shape[1]), lambda i: (i, 0))
     kept = lambda shape: pl.BlockSpec(shape, lambda i: (0, 0))
@@ -225,8 +227,11 @@
         grid=(rows // block,),
         in_specs=[row_block(x) for x in (base, wide_low, wide_hidden)]
         + [kept(x.shape) for x in whole],
-        out_specs=[kept(shape) for shape in out_shapes],
-        out_shape=[jax.ShapeDtypeStruct(shape, jnp.float32) for shape in out_shapes],
+        out_specs=[pl.BlockSpec(memory_space=pltpu.VMEM), kept(out_shapes[1])],
+        out_shape=[
+            pltpu.VMEM(out_shapes[0], jnp.float32),
+            jax.ShapeDtypeStruct(out_shapes[1], jnp.float32),
+        ],
         scratch_shapes=[pltpu.VMEM((wide_low.shape[1], width), jnp.float32)],
     )(base, wide_low, wide_hidden, *whole)
 

time: 232 us -> 235 us (1.013)
  local copies, waits for them, and re-layouts: 8 us -> 13.8 us
    unnamed x14 -> x18, local copies, waits for them, and re-layouts: 0.03 us -> 5.84 us
    pallas_call x1, Pallas kernels: 9.47 us -> 6.98 us  [pack(): pl.pallas_call(functools.partial(pack_kernel, half, room), grid=(experts...]
where the time goes in v7:
time: 235 us; the launch traced here: 233 us
  waiting for transfers between devices  147 us (63%)
  starting transfers between devices  25.8 us (11%)
  matrix products  25.1 us (11%)
  Pallas kernels  18.2 us (8%)
  local copies, waits for them, and re-layouts  13.8 us (6%)
  between operations  2.63 us (1%)
    all_to_all x2, waiting for transfers between devices, exchange(): return lax.all_to_all(block, AXES, split_axis=0, concat_axis=0, tiled=True)  138 us
    all_to_all x2, starting transfers between devices, exchange(): return lax.all_to_all(block, AXES, split_axis=0, concat_axis=0, tiled=True)  19.7 us
    dot_general x1, matrix products, layer(): up_out = jnp.dot(inputs, gate_up[0, 1], preferred_element_type=jnp.float32)  11.1 us
    dot_general x1, matrix products, layer(): jnp.dot(inputs, gate_up[0, 0], preferred_element_type=jnp.float32)  10.9 us
    ppermute x1, waiting for transfers between devices, layer(): lax.ppermute(jnp.where(own_marked, far_low, extra_back), 'expert', pairs)  7.95 us
    pallas_call x1, Pallas kernels, pack(): pl.pallas_call(functools.partial(pack_kernel, half, room), grid=(experts...  6.98 us
    pallas_call x1, Pallas kernels, finish(): pl.pallas_call(finish_kernel, grid=(rows // block,), in_specs=[row_block(...  6.83 us
    unnamed x18, local copies, waits for them, and re-layouts  5.84 us
  transfers between devices with their start and end apart: 5, of which 4 were waited for; matrix products, arithmetic and copies ran while one was open for 14% of the time, Pallas kernels for 5%

profile of v7, /device:TPU:5, one launch (start us, length us, event | category | flops | bytes accessed | tf_op | source)
XLA Modules:
  0.0 233.0 jit_solution(8011269112140855353)
XLA Ops:
  0.6 0.0 copy-start
  0.7 7.0 %shard_map.104 = (bf16[128,8,5120]{2,1,0:T(8,128)(2,1)S(1)}, bf16[128,8,2048]{2,1,0:T(8,128)(2,1)S(1)}) custom-call(s32[4,128]{1,0:T(4,128)} %bitcast.40, f32[4,128]{1,0:T(4,128)} %bitcast.41, s32[1,128]{1,0:T(1,128)} %bitcast.43, s32[1,128]{1,0:T(1,128)} %bitcast.42, s32[1,1]{1,0:T(1,128)} %bitcast.4.own, bf16[128,4096]{1,0:T(8,128)(2,1)} %tokens.1, ...), custom_call_target="tpu_custom_call" | custom-call | tf_op jit(solution)/shard_map/pallas_call | solution.py:95
  7.6 0.0 copy-start.1
  7.6 3.8 %copy-done.1 = bf16[128,8,5120]{2,1,0:T(8,128)(2,1)} copy-done((bf16[128,8,5120]{2,1,0:T(8,128)(2,1)}, bf16[128,8,5120]{2,1,0:T(8,128)(2,1)S(1)}, u32[]{:S(2)}) %copy-start.1) | copy-done | bytes 10485784
  11.5 2.0 copy-done.2
  13.5 11.2 %all-to-all-start.1 = ((bf16[128,8,5120]{2,1,0:T(8,128)(2,1)}), bf16[128,8,5120]{2,1,0:T(8,128)(2,1)}, u32[]{:S(2)}, u32[]{:S(2)}) async-start(bf16[128,8,5120]{2,1,0:T(8,128)(2,1)} %copy-done.1), calls=%async_computation.1 | async-start | bytes 20971520 | tf_op jit(solution)/shard_map/all_to_all | solution.py:240
  24.6 0.0 copy-done.4
  24.7 2.8 %collective-permute-start = (bf16[32,4096]{1,0:T(8,128)(2,1)S(1)}, bf16[32,4096]{1,0:T(8,128)(2,1)S(1)}, u32[]{:S(2)}, u32[]{:S(2)}) collective-permute-start(bf16[32,4096]{1,0:T(8,128)(2,1)S(1)} %bitcast.39), channel_id=1, source_target_pairs={{0,8},{1,9},{2,10},{3,11},{4,12},{5,13},{6,14},{7,15},{8,0},{9,1},... | collective-permute-start | bytes 786440 | tf_op jit(solution)/shard_map/ppermute | solution.py:254
  27.5 137.2 %all-to-all-done.1 = bf16[128,8,5120]{2,1,0:T(8,128)(2,1)} async-done(((bf16[128,8,5120]{2,1,0:T(8,128)(2,1)}), bf16[128,8,5120]{2,1,0:T(8,128)(2,1)}, u32[]{:S(2)}, u32[]{:S(2)}) %all-to-all-start.1) | async-done | bytes 10485792 | tf_op jit(solution)/shard_map/all_to_all | solution.py:240
  164.7 8.5 %all-to-all-start = ((bf16[128,8,2048]{2,1,0:T(8,128)(2,1)}), bf16[128,8,2048]{2,1,0:T(8,128)(2,1)}, u32[]{:S(2)}, u32[]{:S(2)}) async-start(bf16[128,8,2048]{2,1,0:T(8,128)(2,1)} %copy-done.2), calls=%async_computation | async-start | bytes 8388608 | tf_op jit(solution)/shard_map/all_to_all | solution.py:240
  173.2 10.9 %fusion.1 = f32[1024,768]{1,0:T(8,128)S(1)} fusion(bf16[128,8,5120]{2,1,0:T(8,128)(2,1)} %all-to-all-done.1, bf16[1,2,4096,768]{3,2,1,0:T(8,128)(2,1)} %param.15), kind=kOutput, calls=%fused_computation.2 | convolution fusion | flops 6442450944 | bytes 17825792 | tf_op jit(solution)/shard_map/dot_general | solution.py:270
  184.1 11.1 %multiply_convert_fusion.hidden = bf16[1024,768]{1,0:T(8,128)(2,1)S(1)} fusion(f32[1024,768]{1,0:T(8,128)S(1)} %fusion.1, bf16[1,2,4096,768]{3,2,1,0:T(8,128)(2,1)} %param.15, bf16[128,8,5120]{2,1,0:T(8,128)(2,1)} %all-to-all-done.1), kind=kOutput, calls=%fused_computation.7 | convolution fusion | flops 6447169536 | bytes 19398656 | tf_op jit(solution)/shard_map/dot_general | solution.py:271
  195.2 0.0 copy-start.7
  195.2 1.3 fusion.8.low
  196.5 0.0 copy-done.3
  196.5 4.4 %shard_map.105 = (bf16[1024,64]{1,0:T(8,128)(2,1)}, bf16[1024,768]{1,0:T(8,128)(2,1)}, bf16[256,32]{1,0:T(8,128)(2,1)}, bf16[256,768]{1,0:T(8,128)(2,1)}, bf16[2...) custom-call(bf16[1024,32]{1,0:T(8,128)(2,1)} %fusion.8.low, bf16[1024,768]{1,0:T(8,128)(2,1)} %copy-done.3), custom_call_target="tpu_custom_call" | custom-call | tf_op jit(solution)/shard_map/pallas_call | solution.py:142
  200.9 1.2 slice.22
  203.3 0.0 copy-done.7
  203.3 0.6 dynamic_slice.4
  203.9 3.1 %slice.21 = bf16[128,8,1024]{2,1,0:T(8,128)(2,1)} slice(bf16[128,8,5120]{2,1,0:T(8,128)(2,1)} %all-to-all-done.1), slice={[0:128], [0:8], [4096:5120]} | slice | bytes 4194304 | tf_op jit(solution)/shard_map/slice | solution.py:279
  207.0 3.1 %reshape_reshape.3 = bf16[256,4096]{1,0:T(8,128)(2,1)S(1)} reshape(bf16[128,8,1024]{2,1,0:T(8,128)(2,1)} %slice.21) | data formatting | bytes 4194304 | tf_op jit(solution)/shard_map/reshape;reshape | solution.py:280
  210.7 0.0 collective-permute-done
  210.8 1.3 broadcast_select_fusion
  212.1 2.7 %collective-permute-start.1 = (bf16[256,32]{1,0:T(8,128)(2,1)S(1)}, bf16[256,32]{1,0:T(8,128)(2,1)S(1)}, u32[]{:S(2)}, u32[]{:S(2)}) collective-permute-start(bf16[256,32]{1,0:T(8,128)(2,1)S(1)} %get-tuple-element.22), channel_id=1, source_target_pairs={{0,8},{1,9},{2,10},{3,11},{4,12},{5,13},{6,14},{7,15},{8,0},{9,1},... | collective-permute-start | bytes 49160 | tf_op jit(solution)/shard_map/ppermute | solution.py:285
  214.8 8.0 %collective-permute-done.1.far_back = bf16[256,32]{1,0:T(8,128)(2,1)S(1)} collective-permute-done((bf16[256,32]{1,0:T(8,128)(2,1)S(1)}, bf16[256,32]{1,0:T(8,128)(2,1)S(1)}, u32[]{:S(2)}, u32[]{:S(2)}) %collective-permute-start.1) | collective-permute-done | bytes 16416 | tf_op jit(solution)/shard_map/ppermute | solution.py:285
  222.8 0.0 copy-done.6
  222.8 0.5 fusion.17
  223.2 0.7 collective-permute-start.2
  223.9 0.5 all-to-all-done
  224.4 6.8 %shard_map.106 = (f32[32,4096]{1,0:T(8,128)S(1)}, f32[32,768]{1,0:T(8,128)}) custom-call(bf16[1024,2048]{1,0:T(8,128)(2,1)} %bitcast.5.base, bf16[1024,64]{1,0:T(8,128)(2,1)} %get-tuple-element.14.wide_low, bf16[1024,768]{1,0:T(8,128)(2,1)} %get-tuple-element.15.wide_hidden, bf16[32,4096]{1,0:T(8,128)(2,1)} %bitcast.38, ...), custom_call_target="tpu_custom_call" | custom-call | tf_op jit(solution)/shard_map/pallas_call | solution.py:225
  231.3 0.9 collective-permute-done.2
  232.1 0.9 add_bitcast_fusion
  (9 shorter events, 0.0 us)
Async XLA Ops:
  0.6 194.5 %copy-start = (bf16[1,32,768]{2,1,0:T(8,128)(2,1)S(1)}, bf16[1,32,768]{2,1,0:T(8,128)(2,1)}, u32[]{:S(2)}) copy-start(bf16[1,32,768]{2,1,0:T(8,128)(2,1)} %param.16) | copy-start | bytes 147460
  7.6 3.8 %copy-start.1 = (bf16[128,8,5120]{2,1,0:T(8,128)(2,1)}, bf16[128,8,5120]{2,1,0:T(8,128)(2,1)S(1)}, u32[]{:S(2)}) copy-start(bf16[128,8,5120]{2,1,0:T(8,128)(2,1)S(1)} %get-tuple-element.13) | copy-start | bytes 31457284
  11.5 2.0 copy-start.2
  13.5 11.2 %copy-start.4 = (bf16[1,32,4096]{2,1,0:T(8,128)(2,1)S(1)}, bf16[1,32,4096]{2,1,0:T(8,128)(2,1)}, u32[]{:S(2)}) copy-start(bf16[1,32,4096]{2,1,0:T(8,128)(2,1)} %param.17) | copy-start | bytes 786436
  13.5 151.2 %all-to-all-start.1 = ((bf16[128,8,5120]{2,1,0:T(8,128)(2,1)}), bf16[128,8,5120]{2,1,0:T(8,128)(2,1)}, u32[]{:S(2)}, u32[]{:S(2)}) async-start(bf16[128,8,5120]{2,1,0:T(8,128)(2,1)} %copy-done.1), calls=%async_computation.1 | async-start | bytes 20971520 | tf_op jit(solution)/shard_map/all_to_all | solution.py:240
  24.7 186.1 %collective-permute-start = (bf16[32,4096]{1,0:T(8,128)(2,1)S(1)}, bf16[32,4096]{1,0:T(8,128)(2,1)S(1)}, u32[]{:S(2)}, u32[]{:S(2)}) collective-permute-start(bf16[32,4096]{1,0:T(8,128)(2,1)S(1)} %bitcast.39), channel_id=1, source_target_pairs={{0,8},{1,9},{2,10},{3,11},{4,12},{5,13},{6,14},{7,15},{8,0},{9,1},... | collective-permute-start | bytes 786440 | tf_op jit(solution)/shard_map/ppermute | solution.py:254
  164.7 59.8 %all-to-all-start = ((bf16[128,8,2048]{2,1,0:T(8,128)(2,1)}), bf16[128,8,2048]{2,1,0:T(8,128)(2,1)}, u32[]{:S(2)}, u32[]{:S(2)}) async-start(bf16[128,8,2048]{2,1,0:T(8,128)(2,1)} %copy-done.2), calls=%async_computation | async-start | bytes 8388608 | tf_op jit(solution)/shard_map/all_to_all | solution.py:240
  195.2 1.3 copy-start.3
  195.2 8.1 %copy-start.7 = (s32[128]{0:T(128)S(1)}, s32[128]{0:T(128)}, u32[]{:S(2)}) copy-start(s32[128]{0:T(128)} %param.13) | copy-start | bytes 1540
  207.0 3.8 %copy-start.8 = (bf16[256,32]{1,0:T(8,128)(2,1)S(1)}, bf16[256,32]{1,0:T(8,128)(2,1)}, u32[]{:S(2)}) copy-start(bf16[256,32]{1,0:T(8,128)(2,1)} %get-tuple-element.17) | copy-start | bytes 49156
  207.0 15.8 %copy-start.6 = (bf16[256,32]{1,0:T(8,128)(2,1)S(1)}, bf16[256,32]{1,0:T(8,128)(2,1)}, u32[]{:S(2)}) copy-start(bf16[256,32]{1,0:T(8,128)(2,1)} %get-tuple-element.21) | copy-start | bytes 49156
  212.1 10.7 %collective-permute-start.1 = (bf16[256,32]{1,0:T(8,128)(2,1)S(1)}, bf16[256,32]{1,0:T(8,128)(2,1)S(1)}, u32[]{:S(2)}, u32[]{:S(2)}) collective-permute-start(bf16[256,32]{1,0:T(8,128)(2,1)S(1)} %get-tuple-element.22), channel_id=1, source_target_pairs={{0,8},{1,9},{2,10},{3,11},{4,12},{5,13},{6,14},{7,15},{8,0},{9,1},... | collective-permute-start | bytes 49160 | tf_op jit(solution)/shard_map/ppermute | solution.py:285
  222.8 1.7 copy-start.5
  223.2 8.9 %collective-permute-start.2 = (bf16[32,4096]{1,0:T(8,128)(2,1)S(1)}, bf16[32,4096]{1,0:T(8,128)(2,1)S(1)}, u32[]{:S(2)}, u32[]{:S(2)}) collective-permute-start(bf16[32,4096]{1,0:T(8,128)(2,1)S(1)} %get-tuple-element.24), channel_id=1, source_target_pairs={{0,8},{1,9},{2,10},{3,11},{4,12},{5,13},{6,14},{7,15},{8,0},{9,1},... | collective-permute-start | bytes 786440 | tf_op jit(solution)/shard_map/ppermute | solution.py:288
